TPU v7x, 128 devices: a whole 4x4x4 slice. The times are simulated.
128 devices in a mesh: teacher: 4 (over y_hi, core), seq: 32 (over x, y_lo, z).
Axes of the slice: x: 4, y: 4 (y_hi: 2, y_lo: 2; y = y_hi * 2 + y_lo), z: 4, core: 2. Of those that a mesh axis runs over, the one named last changes fastest.
Arguments:
- activations: bfloat16 [20, 2048, 1536], P('teacher', 'seq'), may hold values from -150 to 150
- teacher_maps: bfloat16 [4, 20, 2048, 1536], P('teacher', None, 'seq'), may hold values from -6 to 6
- projection: bfloat16 [4, 1536, 1536], P('teacher', 'seq'), may hold values from -0.625 to 0.625
- dilated_weight: bfloat16 [1536, 3, 768], P('seq'), may hold values from -0.09375 to 0.09375
- pointwise_weight: bfloat16 [768, 1536], P('seq'), may hold values from -0.21875 to 0.21875
Outputs:
- loss_mean: float32 [], replicated
- dilated_grad: float32 [1536, 3, 768], P('seq')
- pointwise_grad: float32 [768, 1536], P('seq')
All inputs are finite; a program needn't handle non-finite values.
Results may differ from a plain program's by a relative error of at most 0.00081.
Values may be sent and summed in bfloat16 or wider, within the bound.
No kernel may reach another device: no remote copies, remote signals or barrier semaphores. Data moves between devices by JAX's collectives and lax.ppermute only.
A program may use at most 128 MiB of HBM per device.

v0:
```python
import jax
import jax.numpy as jnp
import numpy as np
from jax import lax
from jax.experimental import pallas as pl
from jax.experimental.pallas import tpu as pltpu
from jax.sharding import PartitionSpec as P


TAP_DILATION = 16
AXES = ("teacher", "seq")
SHAPE = (2, 2, 4, 2, 4)
STEPS = (0, -1, 1, 2)

slope_const = 0.7978845608
cubic_const = 0.044715


def pairs_of(move):
    pairs = []
    for source in range(int(np.prod(SHAPE))):
        at = [int(v) for v in np.unravel_index(source, SHAPE)]
        pairs.append((source, int(np.ravel_multi_index(move(*at), SHAPE))))
    return pairs


def along(first, step):
    def move(yh, core, x, yl, z):
        if (core == 0) == first:
            return (yh, core, (x + step) % 4, yl, z)
        return (yh, core, x, yl, (z + step) % 4)

    return pairs_of(move)


CORE = pairs_of(lambda yh, core, x, yl, z: (yh, 1 - core, x, yl, z))
FAR = pairs_of(lambda yh, core, x, yl, z: (1 - yh, core, x, yl, z))
NEAR = pairs_of(lambda yh, core, x, yl, z: (yh, core, x, 1 - yl, z))
FAR_NEAR = pairs_of(lambda yh, core, x, yl, z: (1 - yh, core, x, 1 - yl, z))
RING = {(first, step): along(first, step) for first in (True, False) for step in (1, -1, 2)}


def send(value, pairs):
    return lax.ppermute(value, AXES, pairs)


def gelu_tanh(value):
    inside = slope_const * (value + cubic_const * value * value * value)
    return 0.5 * value * (1.0 + jnp.tanh(inside))


def gelu_slope(value):
    inside = slope_const * (value + cubic_const * value * value * value)
    tangent = jnp.tanh(inside)
    return 0.5 * (1.0 + tangent) + 0.5 * value * (1.0 - tangent * tangent) * slope_const * (
        1.0 + 3.0 * cubic_const * value * value
    )


def block_order(core, x, yl, z):
    first = jnp.where(core == 0, x, z)
    second = jnp.where(core == 0, z, x)
    order = []
    for far in STEPS:
        for near in STEPS:
            for side in (0, 1):
                one = (first + near + 4) % 4
                two = (second + far + 4) % 4
                at_x = jnp.where(core == 0, one, two)
                at_z = jnp.where(core == 0, two, one)
                order.append((at_x * 2 + (yl + side) % 2) * 4 + at_z)
    return jnp.stack(order).astype(jnp.int32)


def concat(*values):
    return jnp.concatenate(values)


def after(value, *earlier):
    return lax.optimization_barrier((value, *earlier))[0]


def ring_gather(value, first):
    return [value] + [send(value, RING[first, step]) for step in (1, -1, 2)]


def power_of(peak):
    return jnp.clip(jnp.floor(jnp.log2(jnp.maximum(peak, 1e-30))) - 13.0, -110.0, 127.0)


def pack(value, power, loss=None):
    rows = jnp.broadcast_to(power, (16, value.shape[1]))
    if loss is not None:
        exponent = jnp.floor(jnp.log2(jnp.maximum(loss, 1e-30)))
        rest = loss * jnp.exp2(-exponent)
        upper = jnp.floor(rest * 512.0) / 512.0
        which = lax.broadcasted_iota(jnp.int32, rows.shape, 0)
        for row, part in enumerate((exponent, upper, (rest - upper) * 1024.0)):
            rows = jnp.where(which == row + 1, part, rows)
    scaled = (value * jnp.exp2(-power)).astype(jnp.float16)
    return concat(scaled, rows.astype(jnp.float16))


def power_in(packed):
    return packed[-16:-15].astype(jnp.float32)


def unpack(packed):
    return packed[:-16].astype(jnp.float32) * jnp.exp2(power_in(packed))


def loss_in(packed):
    exponent, upper, lower = [packed[row : row + 1].astype(jnp.float32) for row in (-15, -14, -13)]
    return jnp.exp2(exponent) * (upper + lower / 1024.0)


def sum_everywhere(value):
    value = value + send(value, CORE)
    value = value + send(value, NEAR) + send(value, FAR) + send(value, FAR_NEAR)
    for first in (True, False):
        value = value + send(value, RING[first, 1]) + send(value, RING[first, -1]) + send(value, RING[first, 2])
    return value


def add_up(own, own_power, arrived):
    power = own_power
    for packed in arrived:
        own = own + unpack(packed)
        power = jnp.maximum(power, power_in(packed))
    return own, power + 2.0


def finish_reduce(own, power, loss):
    rows = own.shape[0] // 8
    arrived = [
        send(pack(own[2 * rows * (i + 1) : 2 * rows * (i + 2)], power, loss), RING[True, step])
        for i, step in enumerate(STEPS[1:])
    ]
    own, power = add_up(own[: 2 * rows], power, arrived)
    loss = loss + sum(loss_in(packed) for packed in arrived)
    keep, give = pack(own[:rows], power, loss), pack(own[rows:], power, loss)
    arrived = [send(give, NEAR), send(keep, FAR), send(give, FAR_NEAR)]
    return add_up(own[:rows], power, arrived)[0], loss + sum(loss_in(packed) for packed in arrived)


def load_blocks(order, pieces, target, sem):
    for index, piece in enumerate(pieces):

        def start(at, carry, index=index, piece=piece):
            row = pl.multiple_of(order[8 * index + at] * 48, 16)
            pltpu.make_async_copy(piece.at[at], target(row), sem).start()
            return carry

        lax.fori_loop(0, 8, start, 0)


def teacher_kernel(order, groups, maps_other, maps_own, *refs):
    count = len(refs) - 4
    other, own, whole, sem = refs[count:]
    width = whole.shape[1]
    each = refs[0].shape[2]
    for part in range(count // 4):
        load_blocks(
            order,
            refs[4 * part : 4 * part + 4],
            lambda row, part=part: whole.at[pl.ds(row, 48), part * each : (part + 1) * each],
            sem,
        )
    pltpu.make_async_copy(whole, whole, sem).wait()

    def columns(i, carry):
        lanes = pl.ds(pl.multiple_of(i * 768, 768), 768)
        for maps, out in ((maps_other, other), (maps_own, own)):
            terms = jnp.dot(maps[0], whole[:, lanes], preferred_element_type=jnp.float32)
            out[:320, lanes] = terms.astype(jnp.bfloat16)
            if out.shape[0] > 320:
                power = power_of(jnp.max(jnp.abs(terms), axis=0, keepdims=True)) + 1.0
                out[320:, lanes] = jnp.broadcast_to(power, (16, 768)).astype(jnp.bfloat16)
        return carry

    lax.fori_loop(0, width // 768, columns, 0)


def teacher_terms(order, groups, maps, pieces, extra):
    rows, depth = maps.shape[1:]
    width = pieces[0].shape[2] * len(pieces) // 4
    return pl.pallas_call(
        teacher_kernel,
        grid_spec=pltpu.PrefetchScalarGridSpec(
            num_scalar_prefetch=2,
            grid=(1,),
            in_specs=[
                pl.BlockSpec((1, rows, depth), lambda i, order, groups: (groups[0], 0, 0)),
                pl.BlockSpec((1, rows, depth), lambda i, order, groups: (groups[1], 0, 0)),
            ]
            + [pl.BlockSpec(memory_space=pl.ANY)] * len(pieces),
            out_specs=[whole_block((rows + extra, width))] * 2,
            scratch_shapes=[pltpu.VMEM((depth, width), jnp.bfloat16), pltpu.SemaphoreType.DMA(())],
        ),
        out_shape=[jax.ShapeDtypeStruct((rows + extra, width), jnp.bfloat16)] * 2,
        compiler_params=pltpu.CompilerParams(vmem_limit_bytes=30 * 2**20),
        name="teacher",
    )(order, groups, maps, maps, *pieces)


def forward_kernel(orders, cores, hidden, inputs, near_own, near_other, *refs):
    pieces = refs[:8]
    preact, activated, base, point, whole, sems = refs[8:]
    for part in range(2):
        load_blocks(
            orders.at[part],
            pieces[4 * part : 4 * part + 4],
            lambda row, part=part: whole.at[part, pl.ds(row, 48), :],
            sems.at[part],
        )

    def half(part, carry):
        pltpu.make_async_copy(whole.at[part], whole.at[part], sems.at[part]).wait()
        core = cores[part]

        def rows_of(pair, inner):
            rows = whole[part, pl.ds(pl.multiple_of(96 * pair, 96), 96), 1152:].astype(jnp.float32)
            for side in range(2):
                point[core, pl.ds(pl.multiple_of(48 * pair, 48), 48), side * 384 : side * 384 + 384] = concat(
                    rows[24 * side : 24 * side + 24], rows[48 + 24 * side : 72 + 24 * side]
                ).astype(jnp.bfloat16)
            return inner

        lax.fori_loop(0, 16, rows_of, 0)
        running = jnp.zeros((320, 384), jnp.float32)
        for k in range(3):
            tap = hidden[:, k * TAP_DILATION : k * TAP_DILATION + 64, :].reshape(320, 1536)
            running = running + jnp.dot(
                tap, whole[part, :, k * 384 : k * 384 + 384], preferred_element_type=jnp.float32
            )
        lanes = pl.ds(pl.multiple_of(core * 384, 128), 384)
        preact[:, lanes] = running
        activated[:, lanes] = gelu_tanh(running).astype(jnp.bfloat16)
        return carry

    lax.fori_loop(0, 2, half, 0)

    def student(part, carry):
        lanes = pl.ds(pl.multiple_of(part * 768, 768), 768)
        near = near_own[:, lanes].astype(jnp.float32) + near_other[:, lanes].astype(jnp.float32)
        base[part] = (
            inputs[:, lanes].astype(jnp.float32)
            + jnp.dot(activated[...], point[part], preferred_element_type=jnp.float32)
        ) - near * 0.25
        return carry

    lax.fori_loop(0, 2, student, 0)


def whole_block(shape):
    return pl.BlockSpec(shape, lambda *i: (0,) * len(shape))


def forward_pass(orders, cores, arrays, pieces):
    outs = [((320, 768), jnp.float32), ((320, 768), jnp.bfloat16)]
    outs += [((2, 320, 768), jnp.float32), ((2, 768, 768), jnp.bfloat16)]
    return pl.pallas_call(
        forward_kernel,
        grid_spec=pltpu.PrefetchScalarGridSpec(
            num_scalar_prefetch=2,
            grid=(1,),
            in_specs=[whole_block(array.shape) for array in arrays]
            + [pl.BlockSpec(memory_space=pl.ANY)] * len(pieces),
            out_specs=[whole_block(shape) for shape, _ in outs],
            scratch_shapes=[
                pltpu.VMEM((2, 1536, 1536), jnp.bfloat16),
                pltpu.SemaphoreType.DMA((2,)),
            ],
        ),
        out_shape=[pltpu.HBM(shape, kind) for shape, kind in outs],
        compiler_params=pltpu.CompilerParams(vmem_limit_bytes=45 * 2**20),
        name="forward",
    )(orders, cores, *arrays, *pieces)


def turn_kernel(order, hidden, hidden_other, out, turned):
    def tap_of(k, carry):
        low = pl.multiple_of(k * TAP_DILATION, TAP_DILATION)
        for part, source in enumerate((hidden, hidden_other)):
            tap = source[:, pl.ds(low, 64), :].reshape(320, 1536)
            turned[:, part * 320 : part * 320 + 320] = tap.T

        def slot(i, inner):
            row = pl.multiple_of(order[i] * 48, 16)
            to = pl.multiple_of(i * 48, 48)
            out[k, pl.ds(to, 48), :] = turned[pl.ds(row, 48), :]
            return inner

        return lax.fori_loop(0, 32, slot, carry)

    lax.fori_loop(0, 3, tap_of, 0)


def turn(order, hidden, hidden_other):
    return pl.pallas_call(
        turn_kernel,
        grid_spec=pltpu.PrefetchScalarGridSpec(
            num_scalar_prefetch=1,
            grid=(1,),
            in_specs=[whole_block(hidden.shape)] * 2,
            out_specs=whole_block((3, 1536, 640)),
            scratch_shapes=[pltpu.VMEM((1536, 640), jnp.bfloat16)],
        ),
        out_shape=pltpu.HBM((3, 1536, 640), jnp.bfloat16),
        compiler_params=pltpu.CompilerParams(vmem_limit_bytes=30 * 2**20),
        name="turn",
    )(order, hidden, hidden_other)


def turn_act_kernel(order, activated, activated_other, out, turned):
    turned[:, :320] = activated[...].astype(jnp.float32).T
    turned[:, 320:] = activated_other[...].astype(jnp.float32).T

    def pair(i, carry):
        rows = [turned[pl.ds(pl.multiple_of(order[2 * i + j] * 24, 8), 24), :] for j in range(2)]
        out[pl.ds(pl.multiple_of(i * 48, 48), 48), :] = concat(*rows).astype(jnp.bfloat16)
        return carry

    lax.fori_loop(0, 16, pair, 0)


def turn_act(order, activated, activated_other):
    return pl.pallas_call(
        turn_act_kernel,
        grid_spec=pltpu.PrefetchScalarGridSpec(
            num_scalar_prefetch=1,
            grid=(1,),
            in_specs=[whole_block(activated.shape)] * 2,
            out_specs=whole_block((768, 640)),
            scratch_shapes=[pltpu.VMEM((768, 640), jnp.float32)],
        ),
        out_shape=jax.ShapeDtypeStruct((768, 640), jnp.bfloat16),
        compiler_params=pltpu.CompilerParams(vmem_limit_bytes=16 * 2**20),
        name="turn_act",
    )(order, activated, activated_other)


def gradient_kernel(turned, turned_act, pre, out_grad, out, scratch):
    def scale(lanes, peak):
        power = power_of(peak)
        out[384:, lanes] = jnp.broadcast_to(power, (16, 384))
        return jnp.exp2(-power)

    def tap_of(k, carry):
        product = jnp.dot(turned[k], pre[...], preferred_element_type=jnp.float32)
        lanes = pl.ds(pl.multiple_of(k * 384, 384), 384)
        out[:384, lanes] = product * scale(lanes, jnp.max(jnp.abs(product), axis=0, keepdims=True))
        return carry

    lax.fori_loop(0, 3, tap_of, 0)
    product = jnp.dot(turned_act[...], out_grad[...], preferred_element_type=jnp.float32)
    scratch[...] = product
    peak = jnp.max(jnp.abs(product), axis=0, keepdims=True)
    factor = scale(slice(1152, 1536), jnp.maximum(peak[:, :384], peak[:, 384:]))

    def rows_of(i, carry):
        rows = scratch[pl.ds(pl.multiple_of(24 * i, 8), 24), :]
        to = pl.multiple_of(48 * i, 8)
        out[pl.ds(to, 24), 1152:] = rows[:, :384] * factor
        out[pl.ds(to + 24, 24), 1152:] = rows[:, 384:] * factor
        return carry

    lax.fori_loop(0, 8, rows_of, 0)


def gradient_chunk(index, turned, turned_act, pre, out_grad):
    return pl.pallas_call(
        gradient_kernel,
        grid=(1,),
        in_specs=[
            pl.BlockSpec((3, 384, 640), lambda i: (0, index, 0)),
            pl.BlockSpec((192, 640), lambda i: (index, 0)),
            whole_block(pre.shape),
            whole_block(out_grad.shape),
        ],
        out_specs=pl.BlockSpec(memory_space=pltpu.VMEM),
        out_shape=pltpu.VMEM((400, 1536), jnp.float32),
        scratch_shapes=[pltpu.VMEM((192, 768), jnp.float32)],
        compiler_params=pltpu.CompilerParams(vmem_limit_bytes=20 * 2**20),
        name="gradient",
    )(turned, turned_act, pre, out_grad)


def in_order(core, own, other, axis):
    return jnp.where(
        core == 0,
        jnp.concatenate([own, other], axis=axis),
        jnp.concatenate([other, own], axis=axis),
    )


def half_of(value, index, axis):
    size = value.shape[axis] // 2
    return lax.dynamic_slice_in_dim(value, index * size, size, axis)


def shards(activations, teacher_maps, projection, dilated_weight, pointwise_weight):
    teacher = lax.axis_index("teacher")
    seq = lax.axis_index("seq")
    yh, core = teacher // 2, teacher % 2
    x, yl, z = seq // 8, (seq // 4) % 2, seq % 4
    wins, bins, channels = activations.shape
    rows = wins * bins
    total_rows = rows * 128
    branch = dilated_weight.shape[2]
    half = branch // 2
    inputs = activations.reshape(rows, channels)
    forward = [(g * 32 + i, g * 32 + i + 1) for g in range(4) for i in range(31)]
    backward = [(b, a) for a, b in forward]
    low = send(activations[:, -TAP_DILATION:], forward)
    high = send(activations[:, :TAP_DILATION], backward)
    padded = jnp.concatenate([low, activations, high], axis=1)
    padded_other = send(padded, CORE)
    order = block_order(core, x, yl, z)
    order_other = block_order(1 - core, x, yl, z)
    cores = jnp.stack([core, 1 - core]).astype(jnp.int32)

    own_dil = lax.dynamic_slice_in_dim(dilated_weight, core * half, half, 2).reshape(48, 3 * half)
    own_pw = half_of(pointwise_weight, core, 1)
    own_block = jnp.concatenate([own_dil, concat(own_pw[:, :half], own_pw[:, half:])], axis=1)

    wide = channels // 2
    block = jnp.concatenate([projection[0], own_block], axis=1)[None]
    near = concat(block, send(block, NEAR))
    first = ring_gather(near, True)
    first_a, first_b, first_w = [
        concat(*[v[:, :, low:high] for v in first])
        for low, high in ((0, wide), (wide, channels), (channels, 2 * channels))
    ]
    pieces_a = ring_gather(first_a, False)
    pieces_b = ring_gather(first_b, False)
    pieces_w = ring_gather(first_w, False)
    pieces_other = [send(pieces_w[0], CORE)]
    pieces_other += [send(piece, CORE) for piece in pieces_w[1:]]

    inputs_f = inputs.astype(jnp.float32)
    local = jnp.concatenate([jnp.sum(inputs_f, axis=0), jnp.sum(inputs_f * inputs_f, axis=0)])
    sums = sum_everywhere(local.reshape(24, 128)).reshape(2, channels)
    channel_mean = sums[0] / total_rows
    channel_var = sums[1] / total_rows - channel_mean * channel_mean
    scale = lax.rsqrt(channel_var + 1e-05)
    place = lax.broadcasted_iota(jnp.int32, (1, bins + 2 * TAP_DILATION, 1), 1) + seq * bins
    inside = (place >= TAP_DILATION) & (place < 32 * bins + TAP_DILATION)

    def hidden_of(value):
        normed = (value.astype(jnp.float32) - channel_mean) * scale
        return jnp.where(inside, gelu_tanh(normed), 0.0).astype(jnp.bfloat16)

    hidden, hidden_other = hidden_of(padded), hidden_of(padded_other)

    maps = teacher_maps.reshape(4, rows, teacher_maps.shape[3])
    far_groups = jnp.stack([(1 - yh) * 2 + 1 - core, (1 - yh) * 2 + core]).astype(jnp.int32)
    near_groups = jnp.stack([yh * 2 + 1 - core, yh * 2 + core]).astype(jnp.int32)
    arrived = []
    for pieces in (pieces_a, pieces_b):
        other, own = teacher_terms(order, far_groups, maps, pieces, 16)
        other = send(other, CORE)
        power = jnp.maximum(own[320:321], other[320:321]).astype(jnp.float32)
        packed = pack(own[:320].astype(jnp.float32) + other[:320].astype(jnp.float32), power)
        arrived.append(send(packed, FAR))
    other, own = teacher_terms(order, near_groups, maps, pieces_a + pieces_b, 0)

    other = send(other, CORE)

    preact, activated, base, point = forward_pass(
        jnp.stack([order, order_other]), cores, [hidden, inputs, own, other], pieces_w + pieces_other
    )
    out_grads, squared = [], []
    for value, terms in zip(base, arrived, strict=True):
        misfit = value - unpack(terms) * 0.25
        squared.append(jnp.sum(misfit * misfit, axis=0))
        out_grads.append((misfit / channels).astype(jnp.bfloat16))
    back_grad = sum(
        lax.dot_general(v, w, (((1,), (1,)), ((), ())), preferred_element_type=jnp.float32)
        for v, w in zip(out_grads, point, strict=True)
    )
    preact_grad = (back_grad * gelu_slope(preact)).astype(jnp.bfloat16)

    turned = turn(order, hidden, hidden_other)
    turned_act = turn_act(order, activated, send(activated, CORE))
    out_own = jnp.where(core == 0, *out_grads)
    swapped = send(
        jnp.concatenate(
            [jnp.where(core == 0, *out_grads[::-1]), half_of(preact_grad, 1 - core, 1)], axis=1
        ),
        CORE,
    )
    out_both = concat(out_own, swapped[:, :wide])
    pre_both = concat(half_of(preact_grad, core, 1), swapped[:, wide:])
    arrived = []
    for index in (3, 1, 2, 0):
        chunk = gradient_chunk(index, turned, turned_act, pre_both, out_both)
        if index:
            arrived.append(send(chunk.astype(jnp.float16), RING[False, STEPS[index]]))
    loss = jnp.broadcast_to(after(concat(*squared), chunk), (8, channels))
    loss = loss + sum(send(loss, RING[False, step]) for step in STEPS[1:])
    block, loss = finish_reduce(*add_up(unpack(chunk), power_in(chunk), arrived), loss[:1])
    other = send(concat(block, jnp.broadcast_to(loss, (8, channels))), CORE)
    loss_mean = 0.5 * jnp.sum(loss + other[48:49]) / (channels * total_rows)
    other = other[:48]

    def dilated_columns(v):
        return v[:, : 3 * half].reshape(48, 3, half)

    def pw_columns(v):
        v = v[:, 3 * half :].reshape(2, branch // 32, half)
        return v.transpose(1, 0, 2).reshape(branch // 32, branch)

    dilated_grad = in_order(core, dilated_columns(block), dilated_columns(other), 2)
    pointwise_grad = in_order(core, pw_columns(block), pw_columns(other), 1)
    return (loss_mean, dilated_grad, pointwise_grad)


def solution(mesh):
    in_specs = (
        P("teacher", "seq", None),
        P("teacher", None, "seq", None),
        P("teacher", "seq", None),
        P("seq", None, None),
        P("seq", None),
    )
    out_specs = (P(), P("seq", None, None), P("seq", None))

    return jax.shard_map(shards, mesh=mesh, in_specs=in_specs, out_specs=out_specs, check_vma=False)
```

profile of v0, /device:TPU:1, one launch (start us, length us, event | category | flops | bytes accessed | tf_op | source)
XLA Modules:
  0.0 263.3 jit_solution(13051048892345135504)
XLA Ops:
  8.9 3.0 %collective-permute-done.12 = bf16[1,48,3072]{2,1,0:T(8,128)(2,1)S(1)} collective-permute-done((bf16[1,48,3072]{2,1,0:T(8,128)(2,1)S(1)}, bf16[1,48,3072]{2,1,0:T(8,128)(2,1)S(1)}, u32[]{:S(2)}, u32[]{:S(2)}) %collective-permute-start.12) | collective-permute-done | bytes 294944 | tf_op jit(solution)/shard_map/ppermute | solution.py:44
  18.6 2.6 collective-permute-start.4
  24.5 2.7 %collective-permute-start.5 = (f32[24,128]{1,0:T(8,128)S(1)}, f32[24,128]{1,0:T(8,128)S(1)}, u32[]{:S(2)}, u32[]{:S(2)}) collective-permute-start(f32[24,128]{1,0:T(8,128)S(1)} %fusion.105), channel_id=1, source_target_pairs={{0,68},{1,69},{2,70},{3,71},{4,64},{5,65},{6,66},{7,67},{8,76},{9,... | collective-permute-start | bytes 36872 | tf_op jit(solution)/shard_map/ppermute | solution.py:44
  27.3 3.3 %collective-permute-done.14 = bf16[2,48,3072]{2,1,0:T(8,128)(2,1)S(1)} collective-permute-done((bf16[2,48,3072]{2,1,0:T(8,128)(2,1)}, bf16[2,48,3072]{2,1,0:T(8,128)(2,1)S(1)}, u32[]{:S(2)}, u32[]{:S(2)}) %collective-permute-start.14) | collective-permute-done | bytes 589856 | tf_op jit(solution)/shard_map/ppermute | solution.py:44
  47.2 5.3 %collective-permute-start.17 = (bf16[8,48,768]{2,1,0:T(8,128)(2,1)S(1)}, bf16[8,48,768]{2,1,0:T(8,128)(2,1)S(1)}, u32[]{:S(2)}, u32[]{:S(2)}) collective-permute-start(bf16[8,48,768]{2,1,0:T(8,128)(2,1)S(1)} %pad_maximum_fusion.4.refs_0_), channel_id=1, source_target_pairs={{0,3},{1,0},{2,1},{3,2},{4,7},{5,4},{6,5},{7,6},{8,11},{9,8},{10,9... | collective-permute-start | bytes 1769480 | tf_op jit(solution)/shard_map/ppermute | solution.py:44
  54.4 5.3 %collective-permute-start.10 = (f32[24,128]{1,0:T(8,128)S(1)}, f32[24,128]{1,0:T(8,128)S(1)}, u32[]{:S(2)}, u32[]{:S(2)}) collective-permute-start(f32[24,128]{1,0:T(8,128)S(1)} %add_add_fusion.1), channel_id=1, source_target_pairs={{0,3},{1,0},{2,1},{3,2},{4,7},{5,4},{6,5},{7,6},{8,11},{9,8},{10,9... | collective-permute-start | bytes 36872 | tf_op jit(solution)/shard_map/ppermute | solution.py:44
  61.8 5.6 %teacher.5 = (bf16[336,768]{1,0:T(8,128)(2,1)S(1)}, bf16[336,768]{1,0:T(8,128)(2,1)S(1)}) custom-call(s32[32]{0:T(128)S(1)} %stack.266.order, s32[2]{0:T(128)S(1)} %pad_add_fusion.3.groups, bf16[4,320,1536]{2,1,0:T(8,128)(2,1)S(1)} %bitcast.126, bf16[4,320,1536]{2,1,0:T(8,128)(2,1)S(1)} %bitcast.127, ...), custom_call_target="tpu_custom_call" | custom-call | tf_op jit(solution)/shard_map/teacher/pallas_call | solution.py:187
  67.5 8.6 %collective-permute-start.32 = (bf16[336,768]{1,0:T(8,128)(2,1)S(1)}, bf16[336,768]{1,0:T(8,128)(2,1)S(1)}, u32[]{:S(2)}, u32[]{:S(2)}) collective-permute-start(bf16[336,768]{1,0:T(8,128)(2,1)S(1)} %get-tuple-element.20), channel_id=1, source_target_pairs={{0,32},{1,33},{2,34},{3,35},{4,36},{5,37},{6,38},{7,39},{8,40},{9,... | collective-permute-start | bytes 1548296 | tf_op jit(solution)/shard_map/ppermute | solution.py:44
  76.3 5.7 %teacher.4 = (bf16[336,768]{1,0:T(8,128)(2,1)S(1)}, bf16[336,768]{1,0:T(8,128)(2,1)S(1)}) custom-call(s32[32]{0:T(128)S(1)} %stack.266.order, s32[2]{0:T(128)S(1)} %pad_add_fusion.3.groups, bf16[4,320,1536]{2,1,0:T(8,128)(2,1)S(1)} %bitcast.128, bf16[4,320,1536]{2,1,0:T(8,128)(2,1)S(1)} %bitcast.129, bf16[8,48,768]{2,1,0:T(8,128)(2,1)S(1)} %pad_maximum_fusion.4.refs_0_, ...), custom_call_target="tpu_custom_call" | custom-call | tf_op jit(solution)/shard_map/teacher/pallas_call | solution.py:187
  83.2 3.9 %collective-permute-start.23 = (bf16[8,48,1536]{2,1,0:T(8,128)(2,1)S(1)}, bf16[8,48,1536]{2,1,0:T(8,128)(2,1)S(1)}, u32[]{:S(2)}, u32[]{:S(2)}) collective-permute-start(bf16[8,48,1536]{2,1,0:T(8,128)(2,1)S(1)} %pad_maximum_fusion.refs_0_), channel_id=1, source_target_pairs={{0,1},{1,2},{2,3},{3,0},{4,5},{5,6},{6,7},{7,4},{8,9},{9,10},{10,1... | collective-permute-start | bytes 3538952 | tf_op jit(solution)/shard_map/ppermute | solution.py:44
  88.3 7.2 %collective-permute-start.25 = (bf16[8,48,1536]{2,1,0:T(8,128)(2,1)S(1)}, bf16[8,48,1536]{2,1,0:T(8,128)(2,1)S(1)}, u32[]{:S(2)}, u32[]{:S(2)}) collective-permute-start(bf16[8,48,1536]{2,1,0:T(8,128)(2,1)S(1)} %pad_maximum_fusion.refs_0_), channel_id=1, source_target_pairs={{0,2},{1,3},{2,0},{3,1},{4,6},{5,7},{6,4},{7,5},{8,10},{9,11},{10,... | collective-permute-start | bytes 3538952 | tf_op jit(solution)/shard_map/ppermute | solution.py:44
  96.2 24.1 %collective-permute-done.11 = f32[24,128]{1,0:T(8,128)S(1)} collective-permute-done((f32[24,128]{1,0:T(8,128)S(1)}, f32[24,128]{1,0:T(8,128)S(1)}, u32[]{:S(2)}, u32[]{:S(2)}) %collective-permute-start.11) | collective-permute-done | bytes 12320 | tf_op jit(solution)/shard_map/ppermute | solution.py:44
  121.4 2.9 %collective-permute-done.9 = f32[24,128]{1,0:T(8,128)S(1)} collective-permute-done((f32[24,128]{1,0:T(8,128)S(1)}, f32[24,128]{1,0:T(8,128)S(1)}, u32[]{:S(2)}, u32[]{:S(2)}) %collective-permute-start.9) | collective-permute-done | bytes 12320 | tf_op jit(solution)/shard_map/ppermute | solution.py:44
  128.3 11.3 %collective-permute-done.33 = f16[336,768]{1,0:T(8,128)(2,1)S(1)} collective-permute-done((f16[336,768]{1,0:T(8,128)(2,1)S(1)}, f16[336,768]{1,0:T(8,128)(2,1)S(1)}, u32[]{:S(2)}, u32[]{:S(2)}) %collective-permute-start.33) | collective-permute-done | bytes 516128 | tf_op jit(solution)/shard_map/ppermute | solution.py:44
  139.6 5.7 %teacher.3 = (bf16[320,1536]{1,0:T(8,128)(2,1)S(1)}, bf16[320,1536]{1,0:T(8,128)(2,1)S(1)}) custom-call(s32[32]{0:T(128)S(1)} %stack.266.order, s32[2]{0:T(128)S(1)} %pad_add_fusion.2.groups, bf16[4,320,1536]{2,1,0:T(8,128)(2,1)S(1)} %bitcast.130, bf16[4,320,1536]{2,1,0:T(8,128)(2,1)S(1)} %bitcast.131, bf16[8,48,768]{2,1,0:T(8,128)(2,1)S(1)} %pad_maximum_fusion.4.refs_0_, ...), custom_call_target="tpu_custom_call" | custom-call | tf_op jit(solution)/shard_map/teacher/pallas_call | solution.py:187
  145.9 3.5 %fusion.11 = (bf16[5,96,1536]{2,1,0:T(8,128)(2,1)S(1)}, bf16[5,96,1536]{2,1,0:T(8,128)(2,1)}) fusion(bf16[5,96,1536]{2,1,0:T(8,128)(2,1)S(1)} %collective-permute-done.34, f32[1536]{0:T(1024)S(1)} %fusion.40, f32[1536]{0:T(1024)S(1)} %fusion.41, pred[96]{0:T(512)(128)(4,1)S(1)} %compare_and_fusion, bf16[5,96,1536]{2,1,0:T(8,128)(2,1)S(1)} %constant_dynamic-update-slice_fusion), kind=kLoop, calls=%fused_computation.13 | loop fusion | flops 19169280 | bytes 5910624 | tf_op jit(solution)/shard_map/convert_element_type | solution.py:452
  151.3 17.2 %forward.1 = (f32[320,768]{1,0:T(8,128)}, bf16[320,768]{1,0:T(8,128)(2,1)}, f32[2,320,768]{2,1,0:T(8,128)}, bf16[2,768,768]{2,1,0:T(8,128)(2,1)}) custom-call(s32[2,32]{1,0:T(2,128)S(1)} %pad_add_fusion.orders, s32[2]{0:T(128)S(1)} %pad_add_fusion.1.cores, bf16[5,96,1536]{2,1,0:T(8,128)(2,1)} %get-tuple-element.90.hidden, bf16[320,1536]{1,0:T(8,128)(2,1)S(1)} %bitcast.132, ...), custom_call_target="tpu_custom_call" | custom-call | tf_op jit(solution)/shard_map/forward/pallas_call | solution.py:262
  174.4 7.5 %turn.1.turned = bf16[3,1536,640]{2,1,0:T(8,128)(2,1)} custom-call(s32[32]{0:T(128)S(1)} %stack.266.order, bf16[5,96,1536]{2,1,0:T(8,128)(2,1)S(1)} %copy-done.5, bf16[5,96,1536]{2,1,0:T(8,128)(2,1)S(1)} %get-tuple-element.89.hidden_other), custom_call_target="tpu_custom_call" | custom-call | tf_op jit(solution)/shard_map/turn/pallas_call | solution.py:300
  191.4 5.3 %collective-permute-start.40 = (f16[400,1536]{1,0:T(8,128)(2,1)S(1)}, f16[400,1536]{1,0:T(8,128)(2,1)S(1)}, u32[]{:S(2)}, u32[]{:S(2)}) collective-permute-start(f16[400,1536]{1,0:T(8,128)(2,1)S(1)} %convert_element_type.247), channel_id=1, source_target_pairs={{0,2},{1,3},{2,0},{3,1},{4,6},{5,7},{6,4},{7,5},{8,10},{9,11},{10,... | collective-permute-start | bytes 3686408 | tf_op jit(solution)/shard_map/ppermute | solution.py:44
  202.9 20.5 %collective-permute-done.37 = f32[8,1536]{1,0:T(8,128)S(1)} collective-permute-done((f32[8,1536]{1,0:T(8,128)S(1)}, f32[8,1536]{1,0:T(8,128)S(1)}, u32[]{:S(2)}, u32[]{:S(2)}) %collective-permute-start.37) | collective-permute-done | bytes 49184 | tf_op jit(solution)/shard_map/ppermute | solution.py:44
  232.0 4.1 %collective-permute-done.43 = f16[112,1536]{1,0:T(8,128)(2,1)S(1)} collective-permute-done((f16[112,1536]{1,0:T(8,128)(2,1)S(1)}, f16[112,1536]{1,0:T(8,128)(2,1)S(1)}, u32[]{:S(2)}, u32[]{:S(2)}) %collective-permute-start.43) | collective-permute-done | bytes 344096 | tf_op jit(solution)/shard_map/ppermute | solution.py:44
  236.1 5.9 %collective-permute-done.44 = f16[112,1536]{1,0:T(8,128)(2,1)S(1)} collective-permute-done((f16[112,1536]{1,0:T(8,128)(2,1)S(1)}, f16[112,1536]{1,0:T(8,128)(2,1)S(1)}, u32[]{:S(2)}, u32[]{:S(2)}) %collective-permute-start.44) | collective-permute-done | bytes 344096 | tf_op jit(solution)/shard_map/ppermute | solution.py:44
  247.3 3.7 %collective-permute-done.47 = f16[64,1536]{1,0:T(8,128)(2,1)S(1)} collective-permute-done((f16[64,1536]{1,0:T(8,128)(2,1)S(1)}, f16[64,1536]{1,0:T(8,128)(2,1)S(1)}, u32[]{:S(2)}, u32[]{:S(2)}) %collective-permute-start.47) | collective-permute-done | bytes 196640 | tf_op jit(solution)/shard_map/ppermute | solution.py:44
  252.8 5.0 %collective-permute-start.49 = (f32[56,1536]{1,0:T(8,128)S(1)}, f32[56,1536]{1,0:T(8,128)S(1)}, u32[]{:S(2)}, u32[]{:S(2)}) collective-permute-start(f32[56,1536]{1,0:T(8,128)S(1)} %pad_maximum_fusion.12), channel_id=1, source_target_pairs={{0,32},{1,33},{2,34},{3,35},{4,36},{5,37},{6,38},{7,39},{8,40},{9,... | collective-permute-start | bytes 1032200 | tf_op jit(solution)/shard_map/ppermute | solution.py:44
  (225 shorter events, 90.1 us)
Async XLA Ops:
  14.9 15.7 %collective-permute-start.14 = (bf16[2,48,3072]{2,1,0:T(8,128)(2,1)}, bf16[2,48,3072]{2,1,0:T(8,128)(2,1)S(1)}, u32[]{:S(2)}, u32[]{:S(2)}) collective-permute-start(bf16[2,48,3072]{2,1,0:T(8,128)(2,1)} %pad_maximum_fusion.2), channel_id=1, source_target_pairs={{0,24},{1,25},{2,26},{3,27},{4,28},{5,29},{6,30},{7,31},{8,0},{9,1... | collective-permute-start | bytes 1769480 | tf_op jit(solution)/shard_map/ppermute | solution.py:44
  17.2 16.8 %collective-permute-start.3 = (f32[24,128]{1,0:T(8,128)S(1)}, f32[24,128]{1,0:T(8,128)S(1)}, u32[]{:S(2)}, u32[]{:S(2)}) collective-permute-start(f32[24,128]{1,0:T(8,128)S(1)} %fusion.105), channel_id=1, source_target_pairs={{0,4},{1,5},{2,6},{3,7},{4,0},{5,1},{6,2},{7,3},{8,12},{9,13},{10,... | collective-permute-start | bytes 36872 | tf_op jit(solution)/shard_map/ppermute | solution.py:44
  18.6 15.4 %collective-permute-start.4 = (f32[24,128]{1,0:T(8,128)S(1)}, f32[24,128]{1,0:T(8,128)S(1)}, u32[]{:S(2)}, u32[]{:S(2)}) collective-permute-start(f32[24,128]{1,0:T(8,128)S(1)} %fusion.105), channel_id=1, source_target_pairs={{0,64},{1,65},{2,66},{3,67},{4,68},{5,69},{6,70},{7,71},{8,72},{9,... | collective-permute-start | bytes 36872 | tf_op jit(solution)/shard_map/ppermute | solution.py:44
  33.0 19.4 %collective-permute-start.19 = (bf16[8,48,768]{2,1,0:T(8,128)(2,1)S(1)}, bf16[8,48,768]{2,1,0:T(8,128)(2,1)S(1)}, u32[]{:S(2)}, u32[]{:S(2)}) collective-permute-start(bf16[8,48,768]{2,1,0:T(8,128)(2,1)S(1)} %pad_maximum_fusion.5.refs_4_.refs_0_), channel_id=1, source_target_pairs={{0,1},{1,2},{2,3},{3,0},{4,5},{5,6},{6,7},{7,4},{8,9},{9,10},{10,1... | collective-permute-start | bytes 1769480 | tf_op jit(solution)/shard_map/ppermute | solution.py:44
  45.6 30.5 %collective-permute-start.16 = (bf16[8,48,768]{2,1,0:T(8,128)(2,1)S(1)}, bf16[8,48,768]{2,1,0:T(8,128)(2,1)S(1)}, u32[]{:S(2)}, u32[]{:S(2)}) collective-permute-start(bf16[8,48,768]{2,1,0:T(8,128)(2,1)S(1)} %pad_maximum_fusion.4.refs_0_), channel_id=1, source_target_pairs={{0,1},{1,2},{2,3},{3,0},{4,5},{5,6},{6,7},{7,4},{8,9},{9,10},{10,1... | collective-permute-start | bytes 1769480 | tf_op jit(solution)/shard_map/ppermute | solution.py:44
  47.2 29.1 %collective-permute-start.17 = (bf16[8,48,768]{2,1,0:T(8,128)(2,1)S(1)}, bf16[8,48,768]{2,1,0:T(8,128)(2,1)S(1)}, u32[]{:S(2)}, u32[]{:S(2)}) collective-permute-start(bf16[8,48,768]{2,1,0:T(8,128)(2,1)S(1)} %pad_maximum_fusion.4.refs_0_), channel_id=1, source_target_pairs={{0,3},{1,0},{2,1},{3,2},{4,7},{5,4},{6,5},{7,6},{8,11},{9,8},{10,9... | collective-permute-start | bytes 1769480 | tf_op jit(solution)/shard_map/ppermute | solution.py:44
  52.4 23.8 %collective-permute-start.18 = (bf16[8,48,768]{2,1,0:T(8,128)(2,1)S(1)}, bf16[8,48,768]{2,1,0:T(8,128)(2,1)S(1)}, u32[]{:S(2)}, u32[]{:S(2)}) collective-permute-start(bf16[8,48,768]{2,1,0:T(8,128)(2,1)S(1)} %pad_maximum_fusion.4.refs_0_), channel_id=1, source_target_pairs={{0,2},{1,3},{2,0},{3,1},{4,6},{5,7},{6,4},{7,5},{8,10},{9,11},{10,... | collective-permute-start | bytes 1769480 | tf_op jit(solution)/shard_map/ppermute | solution.py:44
  54.4 41.6 %collective-permute-start.10 = (f32[24,128]{1,0:T(8,128)S(1)}, f32[24,128]{1,0:T(8,128)S(1)}, u32[]{:S(2)}, u32[]{:S(2)}) collective-permute-start(f32[24,128]{1,0:T(8,128)S(1)} %add_add_fusion.1), channel_id=1, source_target_pairs={{0,3},{1,0},{2,1},{3,2},{4,7},{5,4},{6,5},{7,6},{8,11},{9,8},{10,9... | collective-permute-start | bytes 36872 | tf_op jit(solution)/shard_map/ppermute | solution.py:44
  67.5 19.6 %collective-permute-start.32 = (bf16[336,768]{1,0:T(8,128)(2,1)S(1)}, bf16[336,768]{1,0:T(8,128)(2,1)S(1)}, u32[]{:S(2)}, u32[]{:S(2)}) collective-permute-start(bf16[336,768]{1,0:T(8,128)(2,1)S(1)} %get-tuple-element.20), channel_id=1, source_target_pairs={{0,32},{1,33},{2,34},{3,35},{4,36},{5,37},{6,38},{7,39},{8,40},{9,... | collective-permute-start | bytes 1548296 | tf_op jit(solution)/shard_map/ppermute | solution.py:44
  76.2 49.4 %collective-permute-start.34 = (bf16[5,96,1536]{2,1,0:T(8,128)(2,1)S(1)}, bf16[5,96,1536]{2,1,0:T(8,128)(2,1)S(1)}, u32[]{:S(2)}, u32[]{:S(2)}) collective-permute-start(bf16[5,96,1536]{2,1,0:T(8,128)(2,1)S(1)} %constant_dynamic-update-slice_fusion), channel_id=1, source_target_pairs={{0,32},{1,33},{2,34},{3,35},{4,36},{5,37},{6,38},{7,39},{8,40},{9,... | collective-permute-start | bytes 4423688 | tf_op jit(solution)/shard_map/ppermute | solution.py:44
  83.2 44.3 %collective-permute-start.23 = (bf16[8,48,1536]{2,1,0:T(8,128)(2,1)S(1)}, bf16[8,48,1536]{2,1,0:T(8,128)(2,1)S(1)}, u32[]{:S(2)}, u32[]{:S(2)}) collective-permute-start(bf16[8,48,1536]{2,1,0:T(8,128)(2,1)S(1)} %pad_maximum_fusion.refs_0_), channel_id=1, source_target_pairs={{0,1},{1,2},{2,3},{3,0},{4,5},{5,6},{6,7},{7,4},{8,9},{9,10},{10,1... | collective-permute-start | bytes 3538952 | tf_op jit(solution)/shard_map/ppermute | solution.py:44
  87.1 40.5 %collective-permute-start.24 = (bf16[8,48,1536]{2,1,0:T(8,128)(2,1)S(1)}, bf16[8,48,1536]{2,1,0:T(8,128)(2,1)S(1)}, u32[]{:S(2)}, u32[]{:S(2)}) collective-permute-start(bf16[8,48,1536]{2,1,0:T(8,128)(2,1)S(1)} %pad_maximum_fusion.refs_0_), channel_id=1, source_target_pairs={{0,3},{1,0},{2,1},{3,2},{4,7},{5,4},{6,5},{7,6},{8,11},{9,8},{10,9... | collective-permute-start | bytes 3538952 | tf_op jit(solution)/shard_map/ppermute | solution.py:44
  88.3 39.8 %collective-permute-start.25 = (bf16[8,48,1536]{2,1,0:T(8,128)(2,1)S(1)}, bf16[8,48,1536]{2,1,0:T(8,128)(2,1)S(1)}, u32[]{:S(2)}, u32[]{:S(2)}) collective-permute-start(bf16[8,48,1536]{2,1,0:T(8,128)(2,1)S(1)} %pad_maximum_fusion.refs_0_), channel_id=1, source_target_pairs={{0,2},{1,3},{2,0},{3,1},{4,6},{5,7},{6,4},{7,5},{8,10},{9,11},{10,... | collective-permute-start | bytes 3538952 | tf_op jit(solution)/shard_map/ppermute | solution.py:44
  95.9 24.3 %collective-permute-start.11 = (f32[24,128]{1,0:T(8,128)S(1)}, f32[24,128]{1,0:T(8,128)S(1)}, u32[]{:S(2)}, u32[]{:S(2)}) collective-permute-start(f32[24,128]{1,0:T(8,128)S(1)} %add_add_fusion.1), channel_id=1, source_target_pairs={{0,2},{1,3},{2,0},{3,1},{4,6},{5,7},{6,4},{7,5},{8,10},{9,11},{10,... | collective-permute-start | bytes 36872 | tf_op jit(solution)/shard_map/ppermute | solution.py:44
  124.3 15.3 %collective-permute-start.33 = (f16[336,768]{1,0:T(8,128)(2,1)S(1)}, f16[336,768]{1,0:T(8,128)(2,1)S(1)}, u32[]{:S(2)}, u32[]{:S(2)}) collective-permute-start(f16[336,768]{1,0:T(8,128)(2,1)S(1)} %pad_maximum_fusion.10), channel_id=1, source_target_pairs={{0,64},{1,65},{2,66},{3,67},{4,68},{5,69},{6,70},{7,71},{8,72},{9,... | collective-permute-start | bytes 1548296 | tf_op jit(solution)/shard_map/ppermute | solution.py:44
  125.5 20.3 %collective-permute-start.31 = (f16[336,768]{1,0:T(8,128)(2,1)S(1)}, f16[336,768]{1,0:T(8,128)(2,1)S(1)}, u32[]{:S(2)}, u32[]{:S(2)}) collective-permute-start(f16[336,768]{1,0:T(8,128)(2,1)S(1)} %pad_maximum_fusion.9), channel_id=1, source_target_pairs={{0,64},{1,65},{2,66},{3,67},{4,68},{5,69},{6,70},{7,71},{8,72},{9,... | collective-permute-start | bytes 1548296 | tf_op jit(solution)/shard_map/ppermute | solution.py:44
  127.6 21.9 %collective-permute-start.26 = (bf16[8,48,1536]{2,1,0:T(8,128)(2,1)S(1)}, bf16[8,48,1536]{2,1,0:T(8,128)(2,1)S(1)}, u32[]{:S(2)}, u32[]{:S(2)}) collective-permute-start(bf16[8,48,1536]{2,1,0:T(8,128)(2,1)S(1)} %pad_maximum_fusion.refs_0_), channel_id=1, source_target_pairs={{0,32},{1,33},{2,34},{3,35},{4,36},{5,37},{6,38},{7,39},{8,40},{9,... | collective-permute-start | bytes 3538952 | tf_op jit(solution)/shard_map/ppermute | solution.py:44
  127.7 21.8 %collective-permute-start.27 = (bf16[8,48,1536]{2,1,0:T(8,128)(2,1)S(1)}, bf16[8,48,1536]{2,1,0:T(8,128)(2,1)S(1)}, u32[]{:S(2)}, u32[]{:S(2)}) collective-permute-start(bf16[8,48,1536]{2,1,0:T(8,128)(2,1)S(1)} %collective-permute-done.23.refs_1_), channel_id=1, source_target_pairs={{0,32},{1,33},{2,34},{3,35},{4,36},{5,37},{6,38},{7,39},{8,40},{9,... | collective-permute-start | bytes 3538952 | tf_op jit(solution)/shard_map/ppermute | solution.py:44
  128.2 21.3 %collective-permute-start.28 = (bf16[8,48,1536]{2,1,0:T(8,128)(2,1)S(1)}, bf16[8,48,1536]{2,1,0:T(8,128)(2,1)S(1)}, u32[]{:S(2)}, u32[]{:S(2)}) collective-permute-start(bf16[8,48,1536]{2,1,0:T(8,128)(2,1)S(1)} %collective-permute-done.24.refs_2_), channel_id=1, source_target_pairs={{0,32},{1,33},{2,34},{3,35},{4,36},{5,37},{6,38},{7,39},{8,40},{9,... | collective-permute-start | bytes 3538952 | tf_op jit(solution)/shard_map/ppermute | solution.py:44
  191.4 36.8 %collective-permute-start.40 = (f16[400,1536]{1,0:T(8,128)(2,1)S(1)}, f16[400,1536]{1,0:T(8,128)(2,1)S(1)}, u32[]{:S(2)}, u32[]{:S(2)}) collective-permute-start(f16[400,1536]{1,0:T(8,128)(2,1)S(1)} %convert_element_type.247), channel_id=1, source_target_pairs={{0,2},{1,3},{2,0},{3,1},{4,6},{5,7},{6,4},{7,5},{8,10},{9,11},{10,... | collective-permute-start | bytes 3686408 | tf_op jit(solution)/shard_map/ppermute | solution.py:44
  196.9 31.4 %collective-permute-start.41 = (f16[400,1536]{1,0:T(8,128)(2,1)S(1)}, f16[400,1536]{1,0:T(8,128)(2,1)S(1)}, u32[]{:S(2)}, u32[]{:S(2)}) collective-permute-start(f16[400,1536]{1,0:T(8,128)(2,1)S(1)} %convert_element_type.250), channel_id=1, source_target_pairs={{0,3},{1,0},{2,1},{3,2},{4,7},{5,4},{6,5},{7,6},{8,11},{9,8},{10,9... | collective-permute-start | bytes 3686408 | tf_op jit(solution)/shard_map/ppermute | solution.py:44
  197.1 31.2 %collective-permute-start.42 = (f16[400,1536]{1,0:T(8,128)(2,1)S(1)}, f16[400,1536]{1,0:T(8,128)(2,1)S(1)}, u32[]{:S(2)}, u32[]{:S(2)}) collective-permute-start(f16[400,1536]{1,0:T(8,128)(2,1)S(1)} %convert_element_type.253), channel_id=1, source_target_pairs={{0,1},{1,2},{2,3},{3,0},{4,5},{5,6},{6,7},{7,4},{8,9},{9,10},{10,1... | collective-permute-start | bytes 3686408 | tf_op jit(solution)/shard_map/ppermute | solution.py:44
  201.3 22.1 %collective-permute-start.37 = (f32[8,1536]{1,0:T(8,128)S(1)}, f32[8,1536]{1,0:T(8,128)S(1)}, u32[]{:S(2)}, u32[]{:S(2)}) collective-permute-start(f32[8,1536]{1,0:T(8,128)S(1)} %broadcast_in_dim.143), channel_id=1, source_target_pairs={{0,3},{1,0},{2,1},{3,2},{4,7},{5,4},{6,5},{7,6},{8,11},{9,8},{10,9... | collective-permute-start | bytes 147464 | tf_op jit(solution)/shard_map/ppermute | solution.py:44
  202.6 23.0 %collective-permute-start.38 = (f32[8,1536]{1,0:T(8,128)S(1)}, f32[8,1536]{1,0:T(8,128)S(1)}, u32[]{:S(2)}, u32[]{:S(2)}) collective-permute-start(f32[8,1536]{1,0:T(8,128)S(1)} %broadcast_in_dim.143), channel_id=1, source_target_pairs={{0,1},{1,2},{2,3},{3,0},{4,5},{5,6},{6,7},{7,4},{8,9},{9,10},{10,1... | collective-permute-start | bytes 147464 | tf_op jit(solution)/shard_map/ppermute | solution.py:44
  (48 other events, 332.4 us)
where the time goes:
time: 264 us; the launch traced here: 263 us
  waiting for transfers between devices  89 us (34%)
  starting transfers between devices  88.8 us (34%)
  Pallas kernels  52 us (20%)
  other arithmetic  16.3 us (6%)
  local copies, waits for them, and re-layouts  12.3 us (5%)
  between operations  3.33 us (1%)
    ppermute x50, waiting for transfers between devices, send(): return lax.ppermute(value, AXES, pairs)  89 us
    ppermute x50, starting transfers between devices, send(): return lax.ppermute(value, AXES, pairs)  88.8 us
    pallas_call x1, Pallas kernels, forward_pass(): pl.pallas_call(forward_kernel, grid_spec=pltpu.PrefetchScalarGridSpec(num...  17.2 us
    pallas_call x3, Pallas kernels, teacher_terms(): pl.pallas_call(teacher_kernel, grid_spec=pltpu.PrefetchScalarGridSpec(num...  17 us
    pallas_call x4, Pallas kernels, gradient_chunk(): pl.pallas_call(gradient_kernel, grid=(1,), in_specs=[pl.BlockSpec((3, 384...  8.94 us
    unnamed x42, local copies, waits for them, and re-layouts  8.09 us
    pallas_call x1, Pallas kernels, turn(): pl.pallas_call(turn_kernel, grid_spec=pltpu.PrefetchScalarGridSpec(num_sc...  7.53 us
  transfers between devices with their start and end apart: 50, of which 17 were waited for; matrix products, arithmetic and copies ran while one was open for 5% of the time, Pallas kernels for 11%

commit v1 on v0

--- a/solution.py
+++ b/solution.py
@@ -116,7 +116,8 @@
 
 def sum_everywhere(value):
     value = value + send(value, CORE)
-    value = value + send(value, NEAR) + send(value, FAR) + send(value, FAR_NEAR)
+    value = value + send(value, NEAR)
+    value = value + send(value, FAR)
     for first in (True, False):
         value = value + send(value, RING[first, 1]) + send(value, RING[first, -1]) + send(value, RING[first, 2])
     return value
@@ -154,28 +155,36 @@
         lax.fori_loop(0, 8, start, 0)
 
 
-def teacher_kernel(order, groups, maps_other, maps_own, *refs):
+def teacher_kernel(order, groups, maps, *refs):
     count = len(refs) - 4
     other, own, whole, sem = refs[count:]
     width = whole.shape[1]
     each = refs[0].shape[2]
-    for part in range(count // 4):
-        load_blocks(
-            order,
-            refs[4 * part : 4 * part + 4],
-            lambda row, part=part: whole.at[pl.ds(row, 48), part * each : (part + 1) * each],
-            sem,
-        )
-    pltpu.make_async_copy(whole, whole, sem).wait()
+    step = pl.program_id(0)
+
+    @pl.when(step == 0)
+    def _():
+        for part in range(count // 4):
+            load_blocks(
+                order,
+                refs[4 * part : 4 * part + 4],
+                lambda row, part=part: whole.at[pl.ds(row, 48), part * each : (part + 1) * each],
+                sem,
+            )
+        pltpu.make_async_copy(whole, whole, sem).wait()
 
     def columns(i, carry):
         lanes = pl.ds(pl.multiple_of(i * 768, 768), 768)
-        for maps, out in ((maps_other, other), (maps_own, own)):
-            terms = jnp.dot(maps[0], whole[:, lanes], preferred_element_type=jnp.float32)
-            out[:320, lanes] = terms.astype(jnp.bfloat16)
-            if out.shape[0] > 320:
-                power = power_of(jnp.max(jnp.abs(terms), axis=0, keepdims=True)) + 1.0
-                out[320:, lanes] = jnp.broadcast_to(power, (16, 768)).astype(jnp.bfloat16)
+        terms = jnp.dot(maps[0], whole[:, lanes], preferred_element_type=jnp.float32)
+        power = power_of(jnp.max(jnp.abs(terms), axis=0, keepdims=True)) + 1.0
+        for index, out in enumerate((other, own)):
+
+            @pl.when(step == index)
+            def _(out=out):
+                out[:320, lanes] = terms.astype(jnp.bfloat16)
+                if out.shape[0] > 320:
+                    out[320:, lanes] = jnp.broadcast_to(power, (16, 768)).astype(jnp.bfloat16)
+
         return carry
 
     lax.fori_loop(0, width // 768, columns, 0)
@@ -188,11 +197,8 @@
         teacher_kernel,
         grid_spec=pltpu.PrefetchScalarGridSpec(
             num_scalar_prefetch=2,
-            grid=(1,),
-            in_specs=[
-                pl.BlockSpec((1, rows, depth), lambda i, order, groups: (groups[0], 0, 0)),
-                pl.BlockSpec((1, rows, depth), lambda i, order, groups: (groups[1], 0, 0)),
-            ]
+            grid=(2,),
+            in_specs=[pl.BlockSpec((1, rows, depth), lambda i, order, groups: (groups[i], 0, 0))]
             + [pl.BlockSpec(memory_space=pl.ANY)] * len(pieces),
             out_specs=[whole_block((rows + extra, width))] * 2,
             scratch_shapes=[pltpu.VMEM((depth, width), jnp.bfloat16), pltpu.SemaphoreType.DMA(())],
@@ -200,7 +206,7 @@
         out_shape=[jax.ShapeDtypeStruct((rows + extra, width), jnp.bfloat16)] * 2,
         compiler_params=pltpu.CompilerParams(vmem_limit_bytes=30 * 2**20),
         name="teacher",
-    )(order, groups, maps, maps, *pieces)
+    )(order, groups, maps, *pieces)
 
 
 def forward_kernel(orders, cores, hidden, inputs, near_own, near_other, *refs):
@@ -426,12 +432,13 @@
 
     wide = channels // 2
     block = jnp.concatenate([projection[0], own_block], axis=1)[None]
-    near = concat(block, send(block, NEAR))
-    first = ring_gather(near, True)
-    first_a, first_b, first_w = [
-        concat(*[v[:, :, low:high] for v in first])
-        for low, high in ((0, wide), (wide, channels), (channels, 2 * channels))
+    arrived = send(block, NEAR)
+    near_p, near_w = [
+        concat(block[:, :, low : low + channels], arrived[:, :, low : low + channels]) for low in (0, channels)
     ]
+    first = ring_gather(near_p, True)
+    first_a, first_b = [concat(*[v[:, :, low : low + wide] for v in first]) for low in (0, wide)]
+    first_w = concat(*ring_gather(near_w, True))
     pieces_a = ring_gather(first_a, False)
     pieces_b = ring_gather(first_b, False)
     pieces_w = ring_gather(first_w, False)

time: 264 us -> 274 us (1.038)
  waiting for transfers between devices: 89 us -> 96.4 us
  starting transfers between devices: 88.8 us -> 94.1 us
    ppermute x50 -> x52, waiting for transfers between devices: 89 us -> 96.4 us  [send(): return lax.ppermute(value, AXES, pairs)]
    ppermute x50 -> x52, starting transfers between devices: 88.8 us -> 94.1 us  [send(): return lax.ppermute(value, AXES, pairs)]
    unnamed x42 -> x32, local copies, waits for them, and re-layouts: 8.09 us -> 7.58 us
  transfers between devices with their start and end apart: 50 -> 52, of which waited for: 17 -> 22; matrix products, arithmetic and copies ran while one was open for 5% -> 3% of each run, Pallas kernels for 11% -> 11%
where the time goes in v1:
time: 274 us
  waiting for transfers between devices  96.4 us (35%)
  starting transfers between devices  94.1 us (34%)
  Pallas kernels  53.3 us (19%)
  other arithmetic  14.3 us (5%)
  local copies, waits for them, and re-layouts  9.96 us (4%)
  between operations  4 us (1%)
    ppermute x52, waiting for transfers between devices, send(): return lax.ppermute(value, AXES, pairs)  96.4 us
    ppermute x52, starting transfers between devices, send(): return lax.ppermute(value, AXES, pairs)  94.1 us
    pallas_call x3, Pallas kernels, teacher_terms(): pl.pallas_call(teacher_kernel, grid_spec=pltpu.PrefetchScalarGridSpec(num...  18.2 us
    pallas_call x1, Pallas kernels, forward_pass(): pl.pallas_call(forward_kernel, grid_spec=pltpu.PrefetchScalarGridSpec(num...  17.3 us
    pallas_call x4, Pallas kernels, gradient_chunk(): pl.pallas_call(gradient_kernel, grid=(1,), in_specs=[pl.BlockSpec((3, 384...  8.94 us
    unnamed x32, local copies, waits for them, and re-layouts  7.58 us
    pallas_call x1, Pallas kernels, turn(): pl.pallas_call(turn_kernel, grid_spec=pltpu.PrefetchScalarGridSpec(num_sc...  7.54 us
  transfers between devices with their start and end apart: 52, of which 22 were waited for; matrix products, arithmetic and copies ran while one was open for 3% of the time, Pallas kernels for 11%

profile of v1, /device:TPU:1, one launch (start us, length us, event | category | flops | bytes accessed | tf_op | source)
XLA Modules:
  0.0 273.6 jit_solution(17136052521612507447)
XLA Ops:
  8.8 4.2 %collective-permute-start = (bf16[5,16,1536]{2,1,0:T(8,128)(2,1)}, bf16[5,16,1536]{2,1,0:T(8,128)(2,1)}, u32[]{:S(2)}, u32[]{:S(2)}) collective-permute-start(bf16[5,16,1536]{2,1,0:T(8,128)(2,1)} %get-tuple-element.63), channel_id=1, source_target_pairs={{0,1},{1,2},{2,3},{3,4},{4,5},{5,6},{6,7},{7,8},{8,9},{9,10},{10,1... | collective-permute-start | bytes 737288 | tf_op jit(solution)/shard_map/ppermute | solution.py:44
  15.5 3.3 %collective-permute-start.3 = (f32[24,128]{1,0:T(8,128)S(1)}, f32[24,128]{1,0:T(8,128)S(1)}, u32[]{:S(2)}, u32[]{:S(2)}) collective-permute-start(f32[24,128]{1,0:T(8,128)S(1)} %fusion.106), channel_id=1, source_target_pairs={{0,4},{1,5},{2,6},{3,7},{4,0},{5,1},{6,2},{7,3},{8,12},{9,13},{10,... | collective-permute-start | bytes 36872 | tf_op jit(solution)/shard_map/ppermute | solution.py:44
  18.9 4.9 %collective-permute-done.3 = f32[24,128]{1,0:T(8,128)S(1)} collective-permute-done((f32[24,128]{1,0:T(8,128)S(1)}, f32[24,128]{1,0:T(8,128)S(1)}, u32[]{:S(2)}, u32[]{:S(2)}) %collective-permute-start.3) | collective-permute-done | bytes 12320 | tf_op jit(solution)/shard_map/ppermute | solution.py:44
  35.2 3.2 %collective-permute-done.12 = bf16[2,48,1536]{2,1,0:T(8,128)(2,1)S(1)} collective-permute-done((bf16[2,48,1536]{2,1,0:T(8,128)(2,1)S(1)}, bf16[2,48,1536]{2,1,0:T(8,128)(2,1)S(1)}, u32[]{:S(2)}, u32[]{:S(2)}) %collective-permute-start.12) | collective-permute-done | bytes 294944 | tf_op jit(solution)/shard_map/ppermute | solution.py:44
  49.4 4.9 %collective-permute-done.18.refs_5_.refs_1_ = bf16[8,48,768]{2,1,0:T(8,128)(2,1)S(1)} collective-permute-done((bf16[8,48,768]{2,1,0:T(8,128)(2,1)S(1)}, bf16[8,48,768]{2,1,0:T(8,128)(2,1)S(1)}, u32[]{:S(2)}, u32[]{:S(2)}) %collective-permute-start.18) | collective-permute-done | bytes 589856 | tf_op jit(solution)/shard_map/ppermute | solution.py:44
  56.0 4.6 %collective-permute-done.20.refs_7_.refs_3_ = bf16[8,48,768]{2,1,0:T(8,128)(2,1)S(1)} collective-permute-done((bf16[8,48,768]{2,1,0:T(8,128)(2,1)S(1)}, bf16[8,48,768]{2,1,0:T(8,128)(2,1)S(1)}, u32[]{:S(2)}, u32[]{:S(2)}) %collective-permute-start.20) | collective-permute-done | bytes 589856 | tf_op jit(solution)/shard_map/ppermute | solution.py:44
  63.8 6.0 %teacher.5 = (bf16[336,768]{1,0:T(8,128)(2,1)S(1)}, bf16[336,768]{1,0:T(8,128)(2,1)S(1)}) custom-call(s32[32]{0:T(128)S(1)} %stack.266.order, s32[2]{0:T(128)S(1)} %pad_add_fusion.3.groups, bf16[4,320,1536]{2,1,0:T(8,128)(2,1)S(1)} %bitcast.126, bf16[8,48,768]{2,1,0:T(8,128)(2,1)S(1)} %pad_maximum_fusion.3.refs_4_.refs_0_, ...), custom_call_target="tpu_custom_call" | custom-call | tf_op jit(solution)/shard_map/teacher/pallas_call | solution.py:196
  70.1 15.1 %collective-permute-start.34 = (bf16[336,768]{1,0:T(8,128)(2,1)S(1)}, bf16[336,768]{1,0:T(8,128)(2,1)S(1)}, u32[]{:S(2)}, u32[]{:S(2)}) collective-permute-start(bf16[336,768]{1,0:T(8,128)(2,1)S(1)} %get-tuple-element.20), channel_id=1, source_target_pairs={{0,32},{1,33},{2,34},{3,35},{4,36},{5,37},{6,38},{7,39},{8,40},{9,... | collective-permute-start | bytes 1548296 | tf_op jit(solution)/shard_map/ppermute | solution.py:44
  86.7 6.0 %teacher.4 = (bf16[336,768]{1,0:T(8,128)(2,1)S(1)}, bf16[336,768]{1,0:T(8,128)(2,1)S(1)}) custom-call(s32[32]{0:T(128)S(1)} %stack.266.order, s32[2]{0:T(128)S(1)} %pad_add_fusion.3.groups, bf16[4,320,1536]{2,1,0:T(8,128)(2,1)S(1)} %bitcast.127, bf16[8,48,768]{2,1,0:T(8,128)(2,1)S(1)} %pad_maximum_fusion.2.refs_0_, ...), custom_call_target="tpu_custom_call" | custom-call | tf_op jit(solution)/shard_map/teacher/pallas_call | solution.py:196
  98.5 22.2 %collective-permute-done.8 = f32[24,128]{1,0:T(8,128)S(1)} collective-permute-done((f32[24,128]{1,0:T(8,128)S(1)}, f32[24,128]{1,0:T(8,128)S(1)}, u32[]{:S(2)}, u32[]{:S(2)}) %collective-permute-start.8) | collective-permute-done | bytes 12320 | tf_op jit(solution)/shard_map/ppermute | solution.py:44
  127.7 3.9 %collective-permute-start.28 = (bf16[8,48,1536]{2,1,0:T(8,128)(2,1)S(1)}, bf16[8,48,1536]{2,1,0:T(8,128)(2,1)S(1)}, u32[]{:S(2)}, u32[]{:S(2)}) collective-permute-start(bf16[8,48,1536]{2,1,0:T(8,128)(2,1)S(1)} %constant_dynamic-update-slice_fusion.3.refs_0_), channel_id=1, source_target_pairs={{0,32},{1,33},{2,34},{3,35},{4,36},{5,37},{6,38},{7,39},{8,40},{9,... | collective-permute-start | bytes 3538952 | tf_op jit(solution)/shard_map/ppermute | solution.py:44
  132.0 4.0 %collective-permute-done.35 = f16[336,768]{1,0:T(8,128)(2,1)S(1)} collective-permute-done((f16[336,768]{1,0:T(8,128)(2,1)S(1)}, f16[336,768]{1,0:T(8,128)(2,1)S(1)}, u32[]{:S(2)}, u32[]{:S(2)}) %collective-permute-start.35) | collective-permute-done | bytes 516128 | tf_op jit(solution)/shard_map/ppermute | solution.py:44
  136.0 7.7 %collective-permute-start.31 = (bf16[8,48,1536]{2,1,0:T(8,128)(2,1)S(1)}, bf16[8,48,1536]{2,1,0:T(8,128)(2,1)S(1)}, u32[]{:S(2)}, u32[]{:S(2)}) collective-permute-start(bf16[8,48,1536]{2,1,0:T(8,128)(2,1)S(1)} %collective-permute-done.27.refs_3_), channel_id=1, source_target_pairs={{0,32},{1,33},{2,34},{3,35},{4,36},{5,37},{6,38},{7,39},{8,40},{9,... | collective-permute-start | bytes 3538952 | tf_op jit(solution)/shard_map/ppermute | solution.py:44
  143.8 6.3 %teacher.3 = (bf16[320,1536]{1,0:T(8,128)(2,1)S(1)}, bf16[320,1536]{1,0:T(8,128)(2,1)S(1)}) custom-call(s32[32]{0:T(128)S(1)} %stack.266.order, s32[2]{0:T(128)S(1)} %pad_add_fusion.2.groups, bf16[4,320,1536]{2,1,0:T(8,128)(2,1)S(1)} %bitcast.128, bf16[8,48,768]{2,1,0:T(8,128)(2,1)S(1)} %pad_maximum_fusion.2.refs_0_, ...), custom_call_target="tpu_custom_call" | custom-call | tf_op jit(solution)/shard_map/teacher/pallas_call | solution.py:196
  151.2 3.5 %fusion.11 = (bf16[5,96,1536]{2,1,0:T(8,128)(2,1)S(1)}, bf16[5,96,1536]{2,1,0:T(8,128)(2,1)}) fusion(bf16[5,96,1536]{2,1,0:T(8,128)(2,1)S(1)} %collective-permute-done.36, f32[1536]{0:T(1024)S(1)} %fusion.39, f32[1536]{0:T(1024)S(1)} %fusion.40, pred[96]{0:T(512)(128)(4,1)S(1)} %compare_and_fusion, bf16[5,96,1536]{2,1,0:T(8,128)(2,1)S(1)} %constant_dynamic-update-slice_fusion), kind=kLoop, calls=%fused_computation.13 | loop fusion | flops 19169280 | bytes 5910624 | tf_op jit(solution)/shard_map/convert_element_type | solution.py:459
  156.6 17.3 %forward.1 = (f32[320,768]{1,0:T(8,128)}, bf16[320,768]{1,0:T(8,128)(2,1)}, f32[2,320,768]{2,1,0:T(8,128)}, bf16[2,768,768]{2,1,0:T(8,128)(2,1)}) custom-call(s32[2,32]{1,0:T(2,128)S(1)} %pad_add_fusion.orders, s32[2]{0:T(128)S(1)} %pad_add_fusion.1.cores, bf16[5,96,1536]{2,1,0:T(8,128)(2,1)} %get-tuple-element.96.hidden, bf16[320,1536]{1,0:T(8,128)(2,1)S(1)} %bitcast.129, ...), custom_call_target="tpu_custom_call" | custom-call | tf_op jit(solution)/shard_map/forward/pallas_call | solution.py:268
  179.7 7.5 %turn.1.turned = bf16[3,1536,640]{2,1,0:T(8,128)(2,1)} custom-call(s32[32]{0:T(128)S(1)} %stack.266.order, bf16[5,96,1536]{2,1,0:T(8,128)(2,1)S(1)} %copy-done.4, bf16[5,96,1536]{2,1,0:T(8,128)(2,1)S(1)} %get-tuple-element.95.hidden_other), custom_call_target="tpu_custom_call" | custom-call | tf_op jit(solution)/shard_map/turn/pallas_call | solution.py:306
  206.4 22.3 %collective-permute-done.39 = f32[8,1536]{1,0:T(8,128)S(1)} collective-permute-done((f32[8,1536]{1,0:T(8,128)S(1)}, f32[8,1536]{1,0:T(8,128)S(1)}, u32[]{:S(2)}, u32[]{:S(2)}) %collective-permute-start.39) | collective-permute-done | bytes 49184 | tf_op jit(solution)/shard_map/ppermute | solution.py:44
  229.8 3.3 %collective-permute-done.41 = f32[8,1536]{1,0:T(8,128)S(1)} collective-permute-done((f32[8,1536]{1,0:T(8,128)S(1)}, f32[8,1536]{1,0:T(8,128)S(1)}, u32[]{:S(2)}, u32[]{:S(2)}) %collective-permute-start.41) | collective-permute-done | bytes 49184 | tf_op jit(solution)/shard_map/ppermute | solution.py:44
  234.7 3.3 %collective-permute-start.45 = (f16[112,1536]{1,0:T(8,128)(2,1)S(1)}, f16[112,1536]{1,0:T(8,128)(2,1)S(1)}, u32[]{:S(2)}, u32[]{:S(2)}) collective-permute-start(f16[112,1536]{1,0:T(8,128)(2,1)S(1)} %get-tuple-element.92), channel_id=1, source_target_pairs={{0,24},{1,25},{2,26},{3,27},{4,28},{5,29},{6,30},{7,31},{8,0},{9,1... | collective-permute-start | bytes 1032200 | tf_op jit(solution)/shard_map/ppermute | solution.py:44
  240.3 3.1 %collective-permute-done.45 = f16[112,1536]{1,0:T(8,128)(2,1)S(1)} collective-permute-done((f16[112,1536]{1,0:T(8,128)(2,1)S(1)}, f16[112,1536]{1,0:T(8,128)(2,1)S(1)}, u32[]{:S(2)}, u32[]{:S(2)}) %collective-permute-start.45) | collective-permute-done | bytes 344096 | tf_op jit(solution)/shard_map/ppermute | solution.py:44
  243.5 5.8 %collective-permute-done.46 = f16[112,1536]{1,0:T(8,128)(2,1)S(1)} collective-permute-done((f16[112,1536]{1,0:T(8,128)(2,1)S(1)}, f16[112,1536]{1,0:T(8,128)(2,1)S(1)}, u32[]{:S(2)}, u32[]{:S(2)}) %collective-permute-start.46) | collective-permute-done | bytes 344096 | tf_op jit(solution)/shard_map/ppermute | solution.py:44
  255.9 5.2 %collective-permute-done.49 = f16[64,1536]{1,0:T(8,128)(2,1)S(1)} collective-permute-done((f16[64,1536]{1,0:T(8,128)(2,1)S(1)}, f16[64,1536]{1,0:T(8,128)(2,1)S(1)}, u32[]{:S(2)}, u32[]{:S(2)}) %collective-permute-start.49) | collective-permute-done | bytes 196640 | tf_op jit(solution)/shard_map/ppermute | solution.py:44
  263.0 5.0 %collective-permute-start.51 = (f32[56,1536]{1,0:T(8,128)S(1)}, f32[56,1536]{1,0:T(8,128)S(1)}, u32[]{:S(2)}, u32[]{:S(2)}) collective-permute-start(f32[56,1536]{1,0:T(8,128)S(1)} %pad_maximum_fusion.11), channel_id=1, source_target_pairs={{0,32},{1,33},{2,34},{3,35},{4,36},{5,37},{6,38},{7,39},{8,40},{9,... | collective-permute-start | bytes 1032200 | tf_op jit(solution)/shard_map/ppermute | solution.py:44
  (216 shorter events, 97.1 us)
Async XLA Ops:
  3.3 27.2 %collective-permute-start.11 = (bf16[1,48,3072]{2,1,0:T(8,128)(2,1)S(1)}, bf16[1,48,3072]{2,1,0:T(8,128)(2,1)S(1)}, u32[]{:S(2)}, u32[]{:S(2)}) collective-permute-start(bf16[1,48,3072]{2,1,0:T(8,128)(2,1)S(1)} %maximum_bitcast_fusion), channel_id=1, source_target_pairs={{0,4},{1,5},{2,6},{3,7},{4,0},{5,1},{6,2},{7,3},{8,12},{9,13},{10,... | collective-permute-start | bytes 884744 | tf_op jit(solution)/shard_map/ppermute | solution.py:44
  8.8 35.8 %collective-permute-start = (bf16[5,16,1536]{2,1,0:T(8,128)(2,1)}, bf16[5,16,1536]{2,1,0:T(8,128)(2,1)}, u32[]{:S(2)}, u32[]{:S(2)}) collective-permute-start(bf16[5,16,1536]{2,1,0:T(8,128)(2,1)} %get-tuple-element.63), channel_id=1, source_target_pairs={{0,1},{1,2},{2,3},{3,4},{4,5},{5,6},{6,7},{7,8},{8,9},{9,10},{10,1... | collective-permute-start | bytes 737288 | tf_op jit(solution)/shard_map/ppermute | solution.py:44
  13.0 34.6 %collective-permute-start.1 = (bf16[5,16,1536]{2,1,0:T(8,128)(2,1)}, bf16[5,16,1536]{2,1,0:T(8,128)(2,1)S(1)}, u32[]{:S(2)}, u32[]{:S(2)}) collective-permute-start(bf16[5,16,1536]{2,1,0:T(8,128)(2,1)} %get-tuple-element.62), channel_id=1, source_target_pairs={{1,0},{2,1},{3,2},{4,3},{5,4},{6,5},{7,6},{8,7},{9,8},{10,9},{11,1... | collective-permute-start | bytes 737288 | tf_op jit(solution)/shard_map/ppermute | solution.py:44
  47.3 22.9 %collective-permute-start.15 = (bf16[8,48,768]{2,1,0:T(8,128)(2,1)S(1)}, bf16[8,48,768]{2,1,0:T(8,128)(2,1)S(1)}, u32[]{:S(2)}, u32[]{:S(2)}) collective-permute-start(bf16[8,48,768]{2,1,0:T(8,128)(2,1)S(1)} %pad_maximum_fusion.2.refs_0_), channel_id=1, source_target_pairs={{0,1},{1,2},{2,3},{3,0},{4,5},{5,6},{6,7},{7,4},{8,9},{9,10},{10,1... | collective-permute-start | bytes 1769480 | tf_op jit(solution)/shard_map/ppermute | solution.py:44
  47.7 22.1 %collective-permute-start.22 = (bf16[2,48,1536]{2,1,0:T(8,128)(2,1)S(1)}, bf16[2,48,1536]{2,1,0:T(8,128)(2,1)S(1)}, u32[]{:S(2)}, u32[]{:S(2)}) collective-permute-start(bf16[2,48,1536]{2,1,0:T(8,128)(2,1)S(1)} %pad_maximum_fusion.12), channel_id=1, source_target_pairs={{0,8},{1,9},{2,10},{3,11},{4,12},{5,13},{6,14},{7,15},{8,16},{9,17... | collective-permute-start | bytes 884744 | tf_op jit(solution)/shard_map/ppermute | solution.py:44
  54.3 31.0 %collective-permute-start.16 = (bf16[8,48,768]{2,1,0:T(8,128)(2,1)S(1)}, bf16[8,48,768]{2,1,0:T(8,128)(2,1)S(1)}, u32[]{:S(2)}, u32[]{:S(2)}) collective-permute-start(bf16[8,48,768]{2,1,0:T(8,128)(2,1)S(1)} %pad_maximum_fusion.2.refs_0_), channel_id=1, source_target_pairs={{0,3},{1,0},{2,1},{3,2},{4,7},{5,4},{6,5},{7,6},{8,11},{9,8},{10,9... | collective-permute-start | bytes 1769480 | tf_op jit(solution)/shard_map/ppermute | solution.py:44
  54.4 32.3 %collective-permute-start.17 = (bf16[8,48,768]{2,1,0:T(8,128)(2,1)S(1)}, bf16[8,48,768]{2,1,0:T(8,128)(2,1)S(1)}, u32[]{:S(2)}, u32[]{:S(2)}) collective-permute-start(bf16[8,48,768]{2,1,0:T(8,128)(2,1)S(1)} %pad_maximum_fusion.2.refs_0_), channel_id=1, source_target_pairs={{0,2},{1,3},{2,0},{3,1},{4,6},{5,7},{6,4},{7,5},{8,10},{9,11},{10,... | collective-permute-start | bytes 1769480 | tf_op jit(solution)/shard_map/ppermute | solution.py:44
  60.7 32.0 %collective-permute-start.23 = (bf16[2,48,1536]{2,1,0:T(8,128)(2,1)S(1)}, bf16[2,48,1536]{2,1,0:T(8,128)(2,1)S(1)}, u32[]{:S(2)}, u32[]{:S(2)}) collective-permute-start(bf16[2,48,1536]{2,1,0:T(8,128)(2,1)S(1)} %pad_maximum_fusion.12), channel_id=1, source_target_pairs={{0,24},{1,25},{2,26},{3,27},{4,28},{5,29},{6,30},{7,31},{8,0},{9,1... | collective-permute-start | bytes 884744 | tf_op jit(solution)/shard_map/ppermute | solution.py:44
  69.8 23.5 %collective-permute-start.24 = (bf16[2,48,1536]{2,1,0:T(8,128)(2,1)S(1)}, bf16[2,48,1536]{2,1,0:T(8,128)(2,1)S(1)}, u32[]{:S(2)}, u32[]{:S(2)}) collective-permute-start(bf16[2,48,1536]{2,1,0:T(8,128)(2,1)S(1)} %pad_maximum_fusion.12), channel_id=1, source_target_pairs={{0,16},{1,17},{2,18},{3,19},{4,20},{5,21},{6,22},{7,23},{8,24},{9,... | collective-permute-start | bytes 884744 | tf_op jit(solution)/shard_map/ppermute | solution.py:44
  70.1 24.6 %collective-permute-start.34 = (bf16[336,768]{1,0:T(8,128)(2,1)S(1)}, bf16[336,768]{1,0:T(8,128)(2,1)S(1)}, u32[]{:S(2)}, u32[]{:S(2)}) collective-permute-start(bf16[336,768]{1,0:T(8,128)(2,1)S(1)} %get-tuple-element.20), channel_id=1, source_target_pairs={{0,32},{1,33},{2,34},{3,35},{4,36},{5,37},{6,38},{7,39},{8,40},{9,... | collective-permute-start | bytes 1548296 | tf_op jit(solution)/shard_map/ppermute | solution.py:44
  86.7 40.5 %collective-permute-start.36 = (bf16[5,96,1536]{2,1,0:T(8,128)(2,1)S(1)}, bf16[5,96,1536]{2,1,0:T(8,128)(2,1)S(1)}, u32[]{:S(2)}, u32[]{:S(2)}) collective-permute-start(bf16[5,96,1536]{2,1,0:T(8,128)(2,1)S(1)} %constant_dynamic-update-slice_fusion), channel_id=1, source_target_pairs={{0,32},{1,33},{2,34},{3,35},{4,36},{5,37},{6,38},{7,39},{8,40},{9,... | collective-permute-start | bytes 4423688 | tf_op jit(solution)/shard_map/ppermute | solution.py:44
  93.4 34.3 %collective-permute-start.25 = (bf16[8,48,1536]{2,1,0:T(8,128)(2,1)S(1)}, bf16[8,48,1536]{2,1,0:T(8,128)(2,1)S(1)}, u32[]{:S(2)}, u32[]{:S(2)}) collective-permute-start(bf16[8,48,1536]{2,1,0:T(8,128)(2,1)S(1)} %constant_dynamic-update-slice_fusion.3.refs_0_), channel_id=1, source_target_pairs={{0,1},{1,2},{2,3},{3,0},{4,5},{5,6},{6,7},{7,4},{8,9},{9,10},{10,1... | collective-permute-start | bytes 3538952 | tf_op jit(solution)/shard_map/ppermute | solution.py:44
  94.7 36.8 %collective-permute-start.26 = (bf16[8,48,1536]{2,1,0:T(8,128)(2,1)S(1)}, bf16[8,48,1536]{2,1,0:T(8,128)(2,1)S(1)}, u32[]{:S(2)}, u32[]{:S(2)}) collective-permute-start(bf16[8,48,1536]{2,1,0:T(8,128)(2,1)S(1)} %constant_dynamic-update-slice_fusion.3.refs_0_), channel_id=1, source_target_pairs={{0,3},{1,0},{2,1},{3,2},{4,7},{5,4},{6,5},{7,6},{8,11},{9,8},{10,9... | collective-permute-start | bytes 3538952 | tf_op jit(solution)/shard_map/ppermute | solution.py:44
  96.2 35.5 %collective-permute-start.27 = (bf16[8,48,1536]{2,1,0:T(8,128)(2,1)S(1)}, bf16[8,48,1536]{2,1,0:T(8,128)(2,1)S(1)}, u32[]{:S(2)}, u32[]{:S(2)}) collective-permute-start(bf16[8,48,1536]{2,1,0:T(8,128)(2,1)S(1)} %constant_dynamic-update-slice_fusion.3.refs_0_), channel_id=1, source_target_pairs={{0,2},{1,3},{2,0},{3,1},{4,6},{5,7},{6,4},{7,5},{8,10},{9,11},{10,... | collective-permute-start | bytes 3538952 | tf_op jit(solution)/shard_map/ppermute | solution.py:44
  97.4 23.2 %collective-permute-start.8 = (f32[24,128]{1,0:T(8,128)S(1)}, f32[24,128]{1,0:T(8,128)S(1)}, u32[]{:S(2)}, u32[]{:S(2)}) collective-permute-start(f32[24,128]{1,0:T(8,128)S(1)} %add_add_fusion.1), channel_id=1, source_target_pairs={{0,1},{1,2},{2,3},{3,0},{4,5},{5,6},{6,7},{7,4},{8,9},{9,10},{10,1... | collective-permute-start | bytes 36872 | tf_op jit(solution)/shard_map/ppermute | solution.py:44
  127.2 22.8 %collective-permute-start.33 = (f16[336,768]{1,0:T(8,128)(2,1)S(1)}, f16[336,768]{1,0:T(8,128)(2,1)S(1)}, u32[]{:S(2)}, u32[]{:S(2)}) collective-permute-start(f16[336,768]{1,0:T(8,128)(2,1)S(1)} %pad_maximum_fusion.7), channel_id=1, source_target_pairs={{0,64},{1,65},{2,66},{3,67},{4,68},{5,69},{6,70},{7,71},{8,72},{9,... | collective-permute-start | bytes 1548296 | tf_op jit(solution)/shard_map/ppermute | solution.py:44
  127.7 27.1 %collective-permute-start.28 = (bf16[8,48,1536]{2,1,0:T(8,128)(2,1)S(1)}, bf16[8,48,1536]{2,1,0:T(8,128)(2,1)S(1)}, u32[]{:S(2)}, u32[]{:S(2)}) collective-permute-start(bf16[8,48,1536]{2,1,0:T(8,128)(2,1)S(1)} %constant_dynamic-update-slice_fusion.3.refs_0_), channel_id=1, source_target_pairs={{0,32},{1,33},{2,34},{3,35},{4,36},{5,37},{6,38},{7,39},{8,40},{9,... | collective-permute-start | bytes 3538952 | tf_op jit(solution)/shard_map/ppermute | solution.py:44
  131.5 23.2 %collective-permute-start.29 = (bf16[8,48,1536]{2,1,0:T(8,128)(2,1)S(1)}, bf16[8,48,1536]{2,1,0:T(8,128)(2,1)S(1)}, u32[]{:S(2)}, u32[]{:S(2)}) collective-permute-start(bf16[8,48,1536]{2,1,0:T(8,128)(2,1)S(1)} %collective-permute-done.25.refs_1_), channel_id=1, source_target_pairs={{0,32},{1,33},{2,34},{3,35},{4,36},{5,37},{6,38},{7,39},{8,40},{9,... | collective-permute-start | bytes 3538952 | tf_op jit(solution)/shard_map/ppermute | solution.py:44
  131.6 23.1 %collective-permute-start.30 = (bf16[8,48,1536]{2,1,0:T(8,128)(2,1)S(1)}, bf16[8,48,1536]{2,1,0:T(8,128)(2,1)S(1)}, u32[]{:S(2)}, u32[]{:S(2)}) collective-permute-start(bf16[8,48,1536]{2,1,0:T(8,128)(2,1)S(1)} %collective-permute-done.26.refs_2_), channel_id=1, source_target_pairs={{0,32},{1,33},{2,34},{3,35},{4,36},{5,37},{6,38},{7,39},{8,40},{9,... | collective-permute-start | bytes 3538952 | tf_op jit(solution)/shard_map/ppermute | solution.py:44
  196.8 36.5 %collective-permute-start.42 = (f16[400,1536]{1,0:T(8,128)(2,1)S(1)}, f16[400,1536]{1,0:T(8,128)(2,1)S(1)}, u32[]{:S(2)}, u32[]{:S(2)}) collective-permute-start(f16[400,1536]{1,0:T(8,128)(2,1)S(1)} %convert_element_type.247), channel_id=1, source_target_pairs={{0,2},{1,3},{2,0},{3,1},{4,6},{5,7},{6,4},{7,5},{8,10},{9,11},{10,... | collective-permute-start | bytes 3686408 | tf_op jit(solution)/shard_map/ppermute | solution.py:44
  198.8 34.5 %collective-permute-start.43 = (f16[400,1536]{1,0:T(8,128)(2,1)S(1)}, f16[400,1536]{1,0:T(8,128)(2,1)S(1)}, u32[]{:S(2)}, u32[]{:S(2)}) collective-permute-start(f16[400,1536]{1,0:T(8,128)(2,1)S(1)} %convert_element_type.250), channel_id=1, source_target_pairs={{0,3},{1,0},{2,1},{3,2},{4,7},{5,4},{6,5},{7,6},{8,11},{9,8},{10,9... | collective-permute-start | bytes 3686408 | tf_op jit(solution)/shard_map/ppermute | solution.py:44
  200.9 32.4 %collective-permute-start.44 = (f16[400,1536]{1,0:T(8,128)(2,1)S(1)}, f16[400,1536]{1,0:T(8,128)(2,1)S(1)}, u32[]{:S(2)}, u32[]{:S(2)}) collective-permute-start(f16[400,1536]{1,0:T(8,128)(2,1)S(1)} %convert_element_type.253), channel_id=1, source_target_pairs={{0,1},{1,2},{2,3},{3,0},{4,5},{5,6},{6,7},{7,4},{8,9},{9,10},{10,1... | collective-permute-start | bytes 3686408 | tf_op jit(solution)/shard_map/ppermute | solution.py:44
  203.7 25.0 %collective-permute-start.39 = (f32[8,1536]{1,0:T(8,128)S(1)}, f32[8,1536]{1,0:T(8,128)S(1)}, u32[]{:S(2)}, u32[]{:S(2)}) collective-permute-start(f32[8,1536]{1,0:T(8,128)S(1)} %broadcast_in_dim.143), channel_id=1, source_target_pairs={{0,3},{1,0},{2,1},{3,2},{4,7},{5,4},{6,5},{7,6},{8,11},{9,8},{10,9... | collective-permute-start | bytes 147464 | tf_op jit(solution)/shard_map/ppermute | solution.py:44
  206.4 23.4 %collective-permute-start.40 = (f32[8,1536]{1,0:T(8,128)S(1)}, f32[8,1536]{1,0:T(8,128)S(1)}, u32[]{:S(2)}, u32[]{:S(2)}) collective-permute-start(f32[8,1536]{1,0:T(8,128)S(1)} %broadcast_in_dim.143), channel_id=1, source_target_pairs={{0,1},{1,2},{2,3},{3,0},{4,5},{5,6},{6,7},{7,4},{8,9},{9,10},{10,1... | collective-permute-start | bytes 147464 | tf_op jit(solution)/shard_map/ppermute | solution.py:44
  (41 other events, 271.1 us)

commit v2 on v0

--- a/solution.py
+++ b/solution.py
@@ -114,11 +114,14 @@
     return jnp.exp2(exponent) * (upper + lower / 1024.0)
 
 
-def sum_everywhere(value):
+def sum_everywhere(value, earlier):
     value = value + send(value, CORE)
     value = value + send(value, NEAR) + send(value, FAR) + send(value, FAR_NEAR)
-    for first in (True, False):
-        value = value + send(value, RING[first, 1]) + send(value, RING[first, -1]) + send(value, RING[first, 2])
+    for index, first in ((1, True), (2, False)):
+        arrived = [send(value, RING[first, step]) for step in STEPS[1:]]
+        if index == 1:
+            arrived = lax.optimization_barrier((*arrived, earlier))[:3]
+        value = value + sum(arrived)
     return value
 
 
@@ -272,7 +275,7 @@
                 pltpu.SemaphoreType.DMA((2,)),
             ],
         ),
-        out_shape=[pltpu.HBM(shape, kind) for shape, kind in outs],
+        out_shape=[(pltpu.VMEM if i == 1 else pltpu.HBM)(*out) for i, out in enumerate(outs)],
         compiler_params=pltpu.CompilerParams(vmem_limit_bytes=45 * 2**20),
         name="forward",
     )(orders, cores, *arrays, *pieces)
@@ -414,8 +417,6 @@
     backward = [(b, a) for a, b in forward]
     low = send(activations[:, -TAP_DILATION:], forward)
     high = send(activations[:, :TAP_DILATION], backward)
-    padded = jnp.concatenate([low, activations, high], axis=1)
-    padded_other = send(padded, CORE)
     order = block_order(core, x, yl, z)
     order_other = block_order(1 - core, x, yl, z)
     cores = jnp.stack([core, 1 - core]).astype(jnp.int32)
@@ -438,9 +439,13 @@
     pieces_other = [send(pieces_w[0], CORE)]
     pieces_other += [send(piece, CORE) for piece in pieces_w[1:]]
 
+    low, high = lax.optimization_barrier((low, high, pieces_a[1]))[:2]
+    padded = jnp.concatenate([low, activations, high], axis=1)
+    padded_other = send(padded, CORE)
+
     inputs_f = inputs.astype(jnp.float32)
     local = jnp.concatenate([jnp.sum(inputs_f, axis=0), jnp.sum(inputs_f * inputs_f, axis=0)])
-    sums = sum_everywhere(local.reshape(24, 128)).reshape(2, channels)
+    sums = sum_everywhere(local.reshape(24, 128), first_a).reshape(2, channels)
     channel_mean = sums[0] / total_rows
     channel_var = sums[1] / total_rows - channel_mean * channel_mean
     scale = lax.rsqrt(channel_var + 1e-05)

time: 264 us -> 263 us (level)
  waiting for transfers between devices: 89 us -> 77 us
  starting transfers between devices: 88.8 us -> 99.8 us
  local copies, waits for them, and re-layouts: 12.3 us -> 9.55 us
    ppermute x50, waiting for transfers between devices: 89 us -> 77 us  [send(): return lax.ppermute(value, AXES, pairs)]
    ppermute x50, starting transfers between devices: 88.8 us -> 99.8 us  [send(): return lax.ppermute(value, AXES, pairs)]
    unnamed x42 -> x40, local copies, waits for them, and re-layouts: 8.09 us -> 5.83 us
  transfers between devices with their start and end apart: 50 -> 50, of which waited for: 17 -> 22; matrix products, arithmetic and copies ran while one was open for 5% -> 5% of each run, Pallas kernels for 11% -> 11%
where the time goes in v2:
time: 263 us; the launch traced here: 262 us
  starting transfers between devices  99.8 us (38%)
  waiting for transfers between devices  77 us (29%)
  Pallas kernels  53.8 us (20%)
  other arithmetic  17.3 us (7%)
  local copies, waits for them, and re-layouts  9.55 us (4%)
  between operations  3.28 us (1%)
    ppermute x50, starting transfers between devices, send(): return lax.ppermute(value, AXES, pairs)  99.8 us
    ppermute x50, waiting for transfers between devices, send(): return lax.ppermute(value, AXES, pairs)  77 us
    pallas_call x3, Pallas kernels, teacher_terms(): pl.pallas_call(teacher_kernel, grid_spec=pltpu.PrefetchScalarGridSpec(num...  18.2 us
    pallas_call x1, Pallas kernels, forward_pass(): pl.pallas_call(forward_kernel, grid_spec=pltpu.PrefetchScalarGridSpec(num...  17.6 us
    pallas_call x4, Pallas kernels, gradient_chunk(): pl.pallas_call(gradient_kernel, grid=(1,), in_specs=[pl.BlockSpec((3, 384...  9.11 us
    pallas_call x1, Pallas kernels, turn(): pl.pallas_call(turn_kernel, grid_spec=pltpu.PrefetchScalarGridSpec(num_sc...  7.54 us
    unnamed x40, local copies, waits for them, and re-layouts  5.83 us
  transfers between devices with their start and end apart: 50, of which 22 were waited for; matrix products, arithmetic and copies ran while one was open for 5% of the time, Pallas kernels for 11%

profile of v2, /device:TPU:1, one launch (start us, length us, event | category | flops | bytes accessed | tf_op | source)
XLA Modules:
  0.0 262.2 jit_solution(13452635385841870382)
XLA Ops:
  8.0 3.8 %collective-permute-done.2 = bf16[1,48,3072]{2,1,0:T(8,128)(2,1)S(1)} collective-permute-done((bf16[1,48,3072]{2,1,0:T(8,128)(2,1)S(1)}, bf16[1,48,3072]{2,1,0:T(8,128)(2,1)S(1)}, u32[]{:S(2)}, u32[]{:S(2)}) %collective-permute-start.2) | collective-permute-done | bytes 294944 | tf_op jit(solution)/shard_map/ppermute | solution.py:44
  19.3 5.3 %collective-permute-done.3 = bf16[2,48,3072]{2,1,0:T(8,128)(2,1)S(1)} collective-permute-done((bf16[2,48,3072]{2,1,0:T(8,128)(2,1)}, bf16[2,48,3072]{2,1,0:T(8,128)(2,1)S(1)}, u32[]{:S(2)}, u32[]{:S(2)}) %collective-permute-start.3) | collective-permute-done | bytes 589856 | tf_op jit(solution)/shard_map/ppermute | solution.py:44
  24.6 6.5 %collective-permute-done.4 = bf16[2,48,3072]{2,1,0:T(8,128)(2,1)S(1)} collective-permute-done((bf16[2,48,3072]{2,1,0:T(8,128)(2,1)}, bf16[2,48,3072]{2,1,0:T(8,128)(2,1)S(1)}, u32[]{:S(2)}, u32[]{:S(2)}) %collective-permute-start.4) | collective-permute-done | bytes 589856 | tf_op jit(solution)/shard_map/ppermute | solution.py:44
  40.9 3.2 %collective-permute-start.11 = (f32[24,128]{1,0:T(8,128)S(1)}, f32[24,128]{1,0:T(8,128)S(1)}, u32[]{:S(2)}, u32[]{:S(2)}) collective-permute-start(f32[24,128]{1,0:T(8,128)S(1)} %add_add_fusion.2), channel_id=1, source_target_pairs={{0,24},{1,25},{2,26},{3,27},{4,28},{5,29},{6,30},{7,31},{8,0},{9,1... | collective-permute-start | bytes 36872 | tf_op jit(solution)/shard_map/ppermute | solution.py:44
  54.4 4.7 %collective-permute-done.20.refs_6_.refs_2_ = bf16[8,48,768]{2,1,0:T(8,128)(2,1)S(1)} collective-permute-done((bf16[8,48,768]{2,1,0:T(8,128)(2,1)S(1)}, bf16[8,48,768]{2,1,0:T(8,128)(2,1)S(1)}, u32[]{:S(2)}, u32[]{:S(2)}) %collective-permute-start.20) | collective-permute-done | bytes 589856 | tf_op jit(solution)/shard_map/ppermute | solution.py:44
  61.9 6.0 %teacher.5 = (bf16[336,768]{1,0:T(8,128)(2,1)S(1)}, bf16[336,768]{1,0:T(8,128)(2,1)S(1)}) custom-call(s32[32]{0:T(128)S(1)} %stack.266.order, s32[2]{0:T(128)S(1)} %pad_add_fusion.3.groups, bf16[4,320,1536]{2,1,0:T(8,128)(2,1)S(1)} %bitcast.126, bf16[4,320,1536]{2,1,0:T(8,128)(2,1)S(1)} %bitcast.127, ...), custom_call_target="tpu_custom_call" | custom-call | tf_op jit(solution)/shard_map/teacher/pallas_call | solution.py:190
  67.8 3.9 %collective-permute-done.17.refs_2_ = bf16[8,48,768]{2,1,0:T(8,128)(2,1)S(1)} collective-permute-done((bf16[8,48,768]{2,1,0:T(8,128)(2,1)S(1)}, bf16[8,48,768]{2,1,0:T(8,128)(2,1)S(1)}, u32[]{:S(2)}, u32[]{:S(2)}) %collective-permute-start.17) | collective-permute-done | bytes 589856 | tf_op jit(solution)/shard_map/ppermute | solution.py:44
  71.7 5.1 %collective-permute-start.24 = (bf16[8,48,1536]{2,1,0:T(8,128)(2,1)S(1)}, bf16[8,48,1536]{2,1,0:T(8,128)(2,1)S(1)}, u32[]{:S(2)}, u32[]{:S(2)}) collective-permute-start(bf16[8,48,1536]{2,1,0:T(8,128)(2,1)S(1)} %pad_maximum_fusion.refs_0_), channel_id=1, source_target_pairs={{0,3},{1,0},{2,1},{3,2},{4,7},{5,4},{6,5},{7,6},{8,11},{9,8},{10,9... | collective-permute-start | bytes 3538952 | tf_op jit(solution)/shard_map/ppermute | solution.py:44
  78.0 5.6 %teacher.4 = (bf16[336,768]{1,0:T(8,128)(2,1)S(1)}, bf16[336,768]{1,0:T(8,128)(2,1)S(1)}) custom-call(s32[32]{0:T(128)S(1)} %stack.266.order, s32[2]{0:T(128)S(1)} %pad_add_fusion.3.groups, bf16[4,320,1536]{2,1,0:T(8,128)(2,1)S(1)} %bitcast.128, bf16[4,320,1536]{2,1,0:T(8,128)(2,1)S(1)} %bitcast.129, bf16[8,48,768]{2,1,0:T(8,128)(2,1)S(1)} %pad_maximum_fusion.4.refs_0_, ...), custom_call_target="tpu_custom_call" | custom-call | tf_op jit(solution)/shard_map/teacher/pallas_call | solution.py:190
  83.7 9.7 %collective-permute-start.32 = (bf16[336,768]{1,0:T(8,128)(2,1)S(1)}, bf16[336,768]{1,0:T(8,128)(2,1)S(1)}, u32[]{:S(2)}, u32[]{:S(2)}) collective-permute-start(bf16[336,768]{1,0:T(8,128)(2,1)S(1)} %get-tuple-element.30), channel_id=1, source_target_pairs={{0,32},{1,33},{2,34},{3,35},{4,36},{5,37},{6,38},{7,39},{8,40},{9,... | collective-permute-start | bytes 1548296 | tf_op jit(solution)/shard_map/ppermute | solution.py:44
  96.6 7.1 %collective-permute-done.14 = f32[24,128]{1,0:T(8,128)S(1)} collective-permute-done((f32[24,128]{1,0:T(8,128)S(1)}, f32[24,128]{1,0:T(8,128)S(1)}, u32[]{:S(2)}, u32[]{:S(2)}) %collective-permute-start.14) | collective-permute-done | bytes 12320 | tf_op jit(solution)/shard_map/ppermute | solution.py:44
  103.7 3.3 %collective-permute-start.15 = (f32[24,128]{1,0:T(8,128)S(1)}, f32[24,128]{1,0:T(8,128)S(1)}, u32[]{:S(2)}, u32[]{:S(2)}) collective-permute-start(f32[24,128]{1,0:T(8,128)S(1)} %add_add_fusion.1), channel_id=1, source_target_pairs={{0,1},{1,2},{2,3},{3,0},{4,5},{5,6},{6,7},{7,4},{8,9},{9,10},{10,1... | collective-permute-start | bytes 36872 | tf_op jit(solution)/shard_map/ppermute | solution.py:44
  115.2 11.6 %collective-permute-start.26 = (bf16[8,48,1536]{2,1,0:T(8,128)(2,1)S(1)}, bf16[8,48,1536]{2,1,0:T(8,128)(2,1)S(1)}, u32[]{:S(2)}, u32[]{:S(2)}) collective-permute-start(bf16[8,48,1536]{2,1,0:T(8,128)(2,1)S(1)} %pad_maximum_fusion.refs_0_), channel_id=1, source_target_pairs={{0,32},{1,33},{2,34},{3,35},{4,36},{5,37},{6,38},{7,39},{8,40},{9,... | collective-permute-start | bytes 3538952 | tf_op jit(solution)/shard_map/ppermute | solution.py:44
  127.0 6.8 %collective-permute-start.28 = (bf16[8,48,1536]{2,1,0:T(8,128)(2,1)S(1)}, bf16[8,48,1536]{2,1,0:T(8,128)(2,1)S(1)}, u32[]{:S(2)}, u32[]{:S(2)}) collective-permute-start(bf16[8,48,1536]{2,1,0:T(8,128)(2,1)S(1)} %collective-permute-done.24.refs_2_), channel_id=1, source_target_pairs={{0,32},{1,33},{2,34},{3,35},{4,36},{5,37},{6,38},{7,39},{8,40},{9,... | collective-permute-start | bytes 3538952 | tf_op jit(solution)/shard_map/ppermute | solution.py:44
  133.7 5.5 %collective-permute-start.29 = (bf16[8,48,1536]{2,1,0:T(8,128)(2,1)S(1)}, bf16[8,48,1536]{2,1,0:T(8,128)(2,1)S(1)}, u32[]{:S(2)}, u32[]{:S(2)}) collective-permute-start(bf16[8,48,1536]{2,1,0:T(8,128)(2,1)S(1)} %collective-permute-done.25.refs_3_), channel_id=1, source_target_pairs={{0,32},{1,33},{2,34},{3,35},{4,36},{5,37},{6,38},{7,39},{8,40},{9,... | collective-permute-start | bytes 3538952 | tf_op jit(solution)/shard_map/ppermute | solution.py:44
  139.3 6.6 %teacher.3 = (bf16[320,1536]{1,0:T(8,128)(2,1)S(1)}, bf16[320,1536]{1,0:T(8,128)(2,1)S(1)}) custom-call(s32[32]{0:T(128)S(1)} %stack.266.order, s32[2]{0:T(128)S(1)} %pad_add_fusion.2.groups, bf16[4,320,1536]{2,1,0:T(8,128)(2,1)S(1)} %bitcast.130, bf16[4,320,1536]{2,1,0:T(8,128)(2,1)S(1)} %bitcast.131, bf16[8,48,768]{2,1,0:T(8,128)(2,1)S(1)} %pad_maximum_fusion.4.refs_0_, ...), custom_call_target="tpu_custom_call" | custom-call | tf_op jit(solution)/shard_map/teacher/pallas_call | solution.py:190
  146.1 3.5 %fusion.11 = (bf16[5,96,1536]{2,1,0:T(8,128)(2,1)S(1)}, bf16[5,96,1536]{2,1,0:T(8,128)(2,1)}) fusion(bf16[5,96,1536]{2,1,0:T(8,128)(2,1)S(1)} %collective-permute-done.34, f32[1536]{0:T(1024)S(1)} %fusion.40, f32[1536]{0:T(1024)S(1)} %fusion.41, pred[96]{0:T(512)(128)(4,1)S(1)} %compare_and_fusion, bf16[5,96,1536]{2,1,0:T(8,128)(2,1)S(1)} %constant_dynamic-update-slice_fusion), kind=kLoop, calls=%fused_computation.13 | loop fusion | flops 19169280 | bytes 5910624 | tf_op jit(solution)/shard_map/convert_element_type | solution.py:457
  151.4 17.6 %forward.1 = (f32[320,768]{1,0:T(8,128)}, bf16[320,768]{1,0:T(8,128)(2,1)S(1)}, f32[2,320,768]{2,1,0:T(8,128)}, bf16[2,768,768]{2,1,0:T(8,128)(2,1)}) custom-call(s32[2,32]{1,0:T(2,128)S(1)} %pad_add_fusion.orders, s32[2]{0:T(128)S(1)} %pad_add_fusion.1.cores, bf16[5,96,1536]{2,1,0:T(8,128)(2,1)} %get-tuple-element.100.hidden, ...), custom_call_target="tpu_custom_call" | custom-call | tf_op jit(solution)/shard_map/forward/pallas_call | solution.py:265
  174.7 7.5 %turn.1.turned = bf16[3,1536,640]{2,1,0:T(8,128)(2,1)} custom-call(s32[32]{0:T(128)S(1)} %stack.266.order, bf16[5,96,1536]{2,1,0:T(8,128)(2,1)S(1)} %copy-done.4, bf16[5,96,1536]{2,1,0:T(8,128)(2,1)S(1)} %get-tuple-element.99.hidden_other), custom_call_target="tpu_custom_call" | custom-call | tf_op jit(solution)/shard_map/turn/pallas_call | solution.py:303
  201.7 19.9 %collective-permute-done.37 = f32[8,1536]{1,0:T(8,128)S(1)} collective-permute-done((f32[8,1536]{1,0:T(8,128)S(1)}, f32[8,1536]{1,0:T(8,128)S(1)}, u32[]{:S(2)}, u32[]{:S(2)}) %collective-permute-start.37) | collective-permute-done | bytes 49184 | tf_op jit(solution)/shard_map/ppermute | solution.py:44
  221.5 3.5 %collective-permute-start.39 = (f32[8,1536]{1,0:T(8,128)S(1)}, f32[8,1536]{1,0:T(8,128)S(1)}, u32[]{:S(2)}, u32[]{:S(2)}) collective-permute-start(f32[8,1536]{1,0:T(8,128)S(1)} %broadcast_in_dim.143), channel_id=1, source_target_pairs={{0,2},{1,3},{2,0},{3,1},{4,6},{5,7},{6,4},{7,5},{8,10},{9,11},{10,... | collective-permute-start | bytes 147464 | tf_op jit(solution)/shard_map/ppermute | solution.py:44
  230.6 4.0 %collective-permute-done.43 = f16[112,1536]{1,0:T(8,128)(2,1)S(1)} collective-permute-done((f16[112,1536]{1,0:T(8,128)(2,1)S(1)}, f16[112,1536]{1,0:T(8,128)(2,1)S(1)}, u32[]{:S(2)}, u32[]{:S(2)}) %collective-permute-start.43) | collective-permute-done | bytes 344096 | tf_op jit(solution)/shard_map/ppermute | solution.py:44
  234.6 6.0 %collective-permute-done.44 = f16[112,1536]{1,0:T(8,128)(2,1)S(1)} collective-permute-done((f16[112,1536]{1,0:T(8,128)(2,1)S(1)}, f16[112,1536]{1,0:T(8,128)(2,1)S(1)}, u32[]{:S(2)}, u32[]{:S(2)}) %collective-permute-start.44) | collective-permute-done | bytes 344096 | tf_op jit(solution)/shard_map/ppermute | solution.py:44
  250.0 6.7 %collective-permute-start.49 = (f32[56,1536]{1,0:T(8,128)S(1)}, f32[56,1536]{1,0:T(8,128)S(1)}, u32[]{:S(2)}, u32[]{:S(2)}) collective-permute-start(f32[56,1536]{1,0:T(8,128)S(1)} %pad_maximum_fusion.12), channel_id=1, source_target_pairs={{0,32},{1,33},{2,34},{3,35},{4,36},{5,37},{6,38},{7,39},{8,40},{9,... | collective-permute-start | bytes 1032200 | tf_op jit(solution)/shard_map/ppermute | solution.py:44
  (223 shorter events, 95.5 us)
Async XLA Ops:
  7.0 27.0 %collective-permute-start.7 = (f32[24,128]{1,0:T(8,128)S(1)}, f32[24,128]{1,0:T(8,128)S(1)}, u32[]{:S(2)}, u32[]{:S(2)}) collective-permute-start(f32[24,128]{1,0:T(8,128)S(1)} %pad_maximum_fusion.15), channel_id=1, source_target_pairs={{0,32},{1,33},{2,34},{3,35},{4,36},{5,37},{6,38},{7,39},{8,40},{9,... | collective-permute-start | bytes 36872 | tf_op jit(solution)/shard_map/ppermute | solution.py:44
  15.4 15.6 %collective-permute-start.4 = (bf16[2,48,3072]{2,1,0:T(8,128)(2,1)}, bf16[2,48,3072]{2,1,0:T(8,128)(2,1)S(1)}, u32[]{:S(2)}, u32[]{:S(2)}) collective-permute-start(bf16[2,48,3072]{2,1,0:T(8,128)(2,1)} %pad_maximum_fusion.2), channel_id=1, source_target_pairs={{0,24},{1,25},{2,26},{3,27},{4,28},{5,29},{6,30},{7,31},{8,0},{9,1... | collective-permute-start | bytes 1769480 | tf_op jit(solution)/shard_map/ppermute | solution.py:44
  33.0 20.2 %collective-permute-start.19 = (bf16[8,48,768]{2,1,0:T(8,128)(2,1)S(1)}, bf16[8,48,768]{2,1,0:T(8,128)(2,1)S(1)}, u32[]{:S(2)}, u32[]{:S(2)}) collective-permute-start(bf16[8,48,768]{2,1,0:T(8,128)(2,1)S(1)} %pad_maximum_fusion.5.refs_4_.refs_0_), channel_id=1, source_target_pairs={{0,1},{1,2},{2,3},{3,0},{4,5},{5,6},{6,7},{7,4},{8,9},{9,10},{10,1... | collective-permute-start | bytes 1769480 | tf_op jit(solution)/shard_map/ppermute | solution.py:44
  44.1 15.0 %collective-permute-start.20 = (bf16[8,48,768]{2,1,0:T(8,128)(2,1)S(1)}, bf16[8,48,768]{2,1,0:T(8,128)(2,1)S(1)}, u32[]{:S(2)}, u32[]{:S(2)}) collective-permute-start(bf16[8,48,768]{2,1,0:T(8,128)(2,1)S(1)} %pad_maximum_fusion.5.refs_4_.refs_0_), channel_id=1, source_target_pairs={{0,3},{1,0},{2,1},{3,2},{4,7},{5,4},{6,5},{7,6},{8,11},{9,8},{10,9... | collective-permute-start | bytes 1769480 | tf_op jit(solution)/shard_map/ppermute | solution.py:44
  50.9 20.8 %collective-permute-start.17 = (bf16[8,48,768]{2,1,0:T(8,128)(2,1)S(1)}, bf16[8,48,768]{2,1,0:T(8,128)(2,1)S(1)}, u32[]{:S(2)}, u32[]{:S(2)}) collective-permute-start(bf16[8,48,768]{2,1,0:T(8,128)(2,1)S(1)} %pad_maximum_fusion.4.refs_0_), channel_id=1, source_target_pairs={{0,3},{1,0},{2,1},{3,2},{4,7},{5,4},{6,5},{7,6},{8,11},{9,8},{10,9... | collective-permute-start | bytes 1769480 | tf_op jit(solution)/shard_map/ppermute | solution.py:44
  51.9 19.8 %collective-permute-start.18 = (bf16[8,48,768]{2,1,0:T(8,128)(2,1)S(1)}, bf16[8,48,768]{2,1,0:T(8,128)(2,1)S(1)}, u32[]{:S(2)}, u32[]{:S(2)}) collective-permute-start(bf16[8,48,768]{2,1,0:T(8,128)(2,1)S(1)} %pad_maximum_fusion.4.refs_0_), channel_id=1, source_target_pairs={{0,2},{1,3},{2,0},{3,1},{4,6},{5,7},{6,4},{7,5},{8,10},{9,11},{10,... | collective-permute-start | bytes 1769480 | tf_op jit(solution)/shard_map/ppermute | solution.py:44
  53.2 23.6 %collective-permute-start.6 = (bf16[8,48,768]{2,1,0:T(8,128)(2,1)S(1)}, bf16[8,48,768]{2,1,0:T(8,128)(2,1)S(1)}, u32[]{:S(2)}, u32[]{:S(2)}) collective-permute-start(bf16[8,48,768]{2,1,0:T(8,128)(2,1)S(1)} %pad_maximum_fusion.4.refs_0_), channel_id=1, source_target_pairs={{0,1},{1,2},{2,3},{3,0},{4,5},{5,6},{6,7},{7,4},{8,9},{9,10},{10,1... | collective-permute-start | bytes 1769480 | tf_op jit(solution)/shard_map/ppermute | solution.py:44
  59.1 24.6 %collective-permute-start = (bf16[5,16,1536]{2,1,0:T(8,128)(2,1)S(1)}, bf16[5,16,1536]{2,1,0:T(8,128)(2,1)S(1)}, u32[]{:S(2)}, u32[]{:S(2)}) collective-permute-start(bf16[5,16,1536]{2,1,0:T(8,128)(2,1)S(1)} %copy-done.16), channel_id=1, source_target_pairs={{0,1},{1,2},{2,3},{3,4},{4,5},{5,6},{6,7},{7,8},{8,9},{9,10},{10,1... | collective-permute-start | bytes 737288 | tf_op jit(solution)/shard_map/ppermute | solution.py:44
  60.4 33.0 %collective-permute-start.1 = (bf16[5,16,1536]{2,1,0:T(8,128)(2,1)S(1)}, bf16[5,16,1536]{2,1,0:T(8,128)(2,1)S(1)}, u32[]{:S(2)}, u32[]{:S(2)}) collective-permute-start(bf16[5,16,1536]{2,1,0:T(8,128)(2,1)S(1)} %copy-done.15), channel_id=1, source_target_pairs={{1,0},{2,1},{3,2},{4,3},{5,4},{6,5},{7,6},{8,7},{9,8},{10,9},{11,1... | collective-permute-start | bytes 737288 | tf_op jit(solution)/shard_map/ppermute | solution.py:44
  71.7 42.1 %collective-permute-start.23 = (bf16[8,48,1536]{2,1,0:T(8,128)(2,1)S(1)}, bf16[8,48,1536]{2,1,0:T(8,128)(2,1)S(1)}, u32[]{:S(2)}, u32[]{:S(2)}) collective-permute-start(bf16[8,48,1536]{2,1,0:T(8,128)(2,1)S(1)} %pad_maximum_fusion.refs_0_), channel_id=1, source_target_pairs={{0,1},{1,2},{2,3},{3,0},{4,5},{5,6},{6,7},{7,4},{8,9},{9,10},{10,1... | collective-permute-start | bytes 3538952 | tf_op jit(solution)/shard_map/ppermute | solution.py:44
  71.7 43.5 %collective-permute-start.24 = (bf16[8,48,1536]{2,1,0:T(8,128)(2,1)S(1)}, bf16[8,48,1536]{2,1,0:T(8,128)(2,1)S(1)}, u32[]{:S(2)}, u32[]{:S(2)}) collective-permute-start(bf16[8,48,1536]{2,1,0:T(8,128)(2,1)S(1)} %pad_maximum_fusion.refs_0_), channel_id=1, source_target_pairs={{0,3},{1,0},{2,1},{3,2},{4,7},{5,4},{6,5},{7,6},{8,11},{9,8},{10,9... | collective-permute-start | bytes 3538952 | tf_op jit(solution)/shard_map/ppermute | solution.py:44
  76.8 50.0 %collective-permute-start.25 = (bf16[8,48,1536]{2,1,0:T(8,128)(2,1)S(1)}, bf16[8,48,1536]{2,1,0:T(8,128)(2,1)S(1)}, u32[]{:S(2)}, u32[]{:S(2)}) collective-permute-start(bf16[8,48,1536]{2,1,0:T(8,128)(2,1)S(1)} %pad_maximum_fusion.refs_0_), channel_id=1, source_target_pairs={{0,2},{1,3},{2,0},{3,1},{4,6},{5,7},{6,4},{7,5},{8,10},{9,11},{10,... | collective-permute-start | bytes 3538952 | tf_op jit(solution)/shard_map/ppermute | solution.py:44
  95.6 50.3 %collective-permute-start.34 = (bf16[5,96,1536]{2,1,0:T(8,128)(2,1)S(1)}, bf16[5,96,1536]{2,1,0:T(8,128)(2,1)S(1)}, u32[]{:S(2)}, u32[]{:S(2)}) collective-permute-start(bf16[5,96,1536]{2,1,0:T(8,128)(2,1)S(1)} %constant_dynamic-update-slice_fusion), channel_id=1, source_target_pairs={{0,32},{1,33},{2,34},{3,35},{4,36},{5,37},{6,38},{7,39},{8,40},{9,... | collective-permute-start | bytes 4423688 | tf_op jit(solution)/shard_map/ppermute | solution.py:44
  112.1 14.8 %collective-permute-start.33 = (f16[336,768]{1,0:T(8,128)(2,1)S(1)}, f16[336,768]{1,0:T(8,128)(2,1)S(1)}, u32[]{:S(2)}, u32[]{:S(2)}) collective-permute-start(f16[336,768]{1,0:T(8,128)(2,1)S(1)} %pad_maximum_fusion.10), channel_id=1, source_target_pairs={{0,64},{1,65},{2,66},{3,67},{4,68},{5,69},{6,70},{7,71},{8,72},{9,... | collective-permute-start | bytes 1548296 | tf_op jit(solution)/shard_map/ppermute | solution.py:44
  113.7 20.0 %collective-permute-start.31 = (f16[336,768]{1,0:T(8,128)(2,1)S(1)}, f16[336,768]{1,0:T(8,128)(2,1)S(1)}, u32[]{:S(2)}, u32[]{:S(2)}) collective-permute-start(f16[336,768]{1,0:T(8,128)(2,1)S(1)} %pad_maximum_fusion.9), channel_id=1, source_target_pairs={{0,64},{1,65},{2,66},{3,67},{4,68},{5,69},{6,70},{7,71},{8,72},{9,... | collective-permute-start | bytes 1548296 | tf_op jit(solution)/shard_map/ppermute | solution.py:44
  115.2 34.4 %collective-permute-start.26 = (bf16[8,48,1536]{2,1,0:T(8,128)(2,1)S(1)}, bf16[8,48,1536]{2,1,0:T(8,128)(2,1)S(1)}, u32[]{:S(2)}, u32[]{:S(2)}) collective-permute-start(bf16[8,48,1536]{2,1,0:T(8,128)(2,1)S(1)} %pad_maximum_fusion.refs_0_), channel_id=1, source_target_pairs={{0,32},{1,33},{2,34},{3,35},{4,36},{5,37},{6,38},{7,39},{8,40},{9,... | collective-permute-start | bytes 3538952 | tf_op jit(solution)/shard_map/ppermute | solution.py:44
  126.9 22.7 %collective-permute-start.27 = (bf16[8,48,1536]{2,1,0:T(8,128)(2,1)S(1)}, bf16[8,48,1536]{2,1,0:T(8,128)(2,1)S(1)}, u32[]{:S(2)}, u32[]{:S(2)}) collective-permute-start(bf16[8,48,1536]{2,1,0:T(8,128)(2,1)S(1)} %collective-permute-done.23.refs_1_), channel_id=1, source_target_pairs={{0,32},{1,33},{2,34},{3,35},{4,36},{5,37},{6,38},{7,39},{8,40},{9,... | collective-permute-start | bytes 3538952 | tf_op jit(solution)/shard_map/ppermute | solution.py:44
  127.0 22.7 %collective-permute-start.28 = (bf16[8,48,1536]{2,1,0:T(8,128)(2,1)S(1)}, bf16[8,48,1536]{2,1,0:T(8,128)(2,1)S(1)}, u32[]{:S(2)}, u32[]{:S(2)}) collective-permute-start(bf16[8,48,1536]{2,1,0:T(8,128)(2,1)S(1)} %collective-permute-done.24.refs_2_), channel_id=1, source_target_pairs={{0,32},{1,33},{2,34},{3,35},{4,36},{5,37},{6,38},{7,39},{8,40},{9,... | collective-permute-start | bytes 3538952 | tf_op jit(solution)/shard_map/ppermute | solution.py:44
  133.7 15.9 %collective-permute-start.29 = (bf16[8,48,1536]{2,1,0:T(8,128)(2,1)S(1)}, bf16[8,48,1536]{2,1,0:T(8,128)(2,1)S(1)}, u32[]{:S(2)}, u32[]{:S(2)}) collective-permute-start(bf16[8,48,1536]{2,1,0:T(8,128)(2,1)S(1)} %collective-permute-done.25.refs_3_), channel_id=1, source_target_pairs={{0,32},{1,33},{2,34},{3,35},{4,36},{5,37},{6,38},{7,39},{8,40},{9,... | collective-permute-start | bytes 3538952 | tf_op jit(solution)/shard_map/ppermute | solution.py:44
  191.9 34.7 %collective-permute-start.40 = (f16[400,1536]{1,0:T(8,128)(2,1)S(1)}, f16[400,1536]{1,0:T(8,128)(2,1)S(1)}, u32[]{:S(2)}, u32[]{:S(2)}) collective-permute-start(f16[400,1536]{1,0:T(8,128)(2,1)S(1)} %convert_element_type.247), channel_id=1, source_target_pairs={{0,2},{1,3},{2,0},{3,1},{4,6},{5,7},{6,4},{7,5},{8,10},{9,11},{10,... | collective-permute-start | bytes 3686408 | tf_op jit(solution)/shard_map/ppermute | solution.py:44
  194.1 32.5 %collective-permute-start.41 = (f16[400,1536]{1,0:T(8,128)(2,1)S(1)}, f16[400,1536]{1,0:T(8,128)(2,1)S(1)}, u32[]{:S(2)}, u32[]{:S(2)}) collective-permute-start(f16[400,1536]{1,0:T(8,128)(2,1)S(1)} %convert_element_type.250), channel_id=1, source_target_pairs={{0,3},{1,0},{2,1},{3,2},{4,7},{5,4},{6,5},{7,6},{8,11},{9,8},{10,9... | collective-permute-start | bytes 3686408 | tf_op jit(solution)/shard_map/ppermute | solution.py:44
  196.1 30.6 %collective-permute-start.42 = (f16[400,1536]{1,0:T(8,128)(2,1)S(1)}, f16[400,1536]{1,0:T(8,128)(2,1)S(1)}, u32[]{:S(2)}, u32[]{:S(2)}) collective-permute-start(f16[400,1536]{1,0:T(8,128)(2,1)S(1)} %convert_element_type.253), channel_id=1, source_target_pairs={{0,1},{1,2},{2,3},{3,0},{4,5},{5,6},{6,7},{7,4},{8,9},{9,10},{10,1... | collective-permute-start | bytes 3686408 | tf_op jit(solution)/shard_map/ppermute | solution.py:44
  198.9 22.6 %collective-permute-start.37 = (f32[8,1536]{1,0:T(8,128)S(1)}, f32[8,1536]{1,0:T(8,128)S(1)}, u32[]{:S(2)}, u32[]{:S(2)}) collective-permute-start(f32[8,1536]{1,0:T(8,128)S(1)} %broadcast_in_dim.143), channel_id=1, source_target_pairs={{0,3},{1,0},{2,1},{3,2},{4,7},{5,4},{6,5},{7,6},{8,11},{9,8},{10,9... | collective-permute-start | bytes 147464 | tf_op jit(solution)/shard_map/ppermute | solution.py:44
  201.7 23.4 %collective-permute-start.38 = (f32[8,1536]{1,0:T(8,128)S(1)}, f32[8,1536]{1,0:T(8,128)S(1)}, u32[]{:S(2)}, u32[]{:S(2)}) collective-permute-start(f32[8,1536]{1,0:T(8,128)S(1)} %broadcast_in_dim.143), channel_id=1, source_target_pairs={{0,1},{1,2},{2,3},{3,0},{4,5},{5,6},{6,7},{7,4},{8,9},{9,10},{10,1... | collective-permute-start | bytes 147464 | tf_op jit(solution)/shard_map/ppermute | solution.py:44
  (47 other events, 325.8 us)
